TPU v7x, 128 devices: a whole 4x4x4 slice. The times are simulated.
128 devices in a mesh: period: 4 (over x_hi, core), bus: 32 (over z, x_lo, y).
Axes of the slice: x: 4 (x_hi: 2, x_lo: 2; x = x_hi * 2 + x_lo), y: 4, z: 4, core: 2. Of those that a mesh axis runs over, the one named last changes fastest.
Arguments:
- gain: bfloat16 [4, 2048, 2048], P('period', 'bus'), may hold values from -0.15 to 1.15
- schur: bfloat16 [4, 2048, 2048], P('period', 'bus'), may hold values from -0.0625 to 0.0625
- inverse_blocks: bfloat16 [4, 10240, 320], P('period', 'bus'), may hold values from -0.3125 to 0.3125
- sensitivity: bfloat16 [10240, 2048], P('bus'), may hold values from -0.109375 to 0.109375
- residual_bus: float32 [4, 10240, 512], P('period', 'bus'), may hold values from -6 to 6
- unit_rhs: float32 [4, 2048, 512], P('period', 'bus'), may hold values from -6 to 6
- start_state: float32 [2048, 512], P('bus'), may hold values from -6 to 6
- active_set: int32 [4, 10240], P('period', 'bus'), may hold values 0 or 1
- unit_bus: int32 [2048], replicated, may hold values from 0 to 10239
Outputs:
- storage_path: float32 [4, 2048, 512], P('period', 'bus')
- costate: float32 [4, 2048, 512], P('period', 'bus')
- bus_update: float32 [4, 10240, 512], P('period', 'bus')
All inputs are finite; a program needn't handle non-finite values. No bound on the sum of `active_set` on one device may be relied on, other than what follows from the above.
Results may differ from a plain program's by a relative error of at most 0.008.
Values may be sent and summed in bfloat16 or wider, within the bound.
A program may use at most 64 MiB of HBM per device.

v0:
```python
import jax
import jax.numpy as jnp
from jax import lax
from jax.sharding import PartitionSpec as P


def passed_along(block, axis, distance):
    devices = range(lax.axis_size(axis))
    route = [(i - distance, i) for i in devices if i - distance in devices]
    return lax.ppermute(block, axis, route)


def body(
    gain,
    schur,
    inverse_blocks,
    sensitivity,
    residual_bus,
    unit_rhs,
    start_state,
    active_set,
    unit_bus,
):
    per_dev, unit_rows, total_units = gain.shape
    bus_rows = inverse_blocks.shape[1]
    rhs_cols = residual_bus.shape[2]
    groups = lax.axis_size("period")
    period_rank = lax.axis_index("period")
    bus_rank = lax.axis_index("bus")
    weighted = residual_bus * (1.0 + 3.0 * active_set[:, :, None].astype(jnp.float32))
    net_in = weighted.astype(jnp.bfloat16)
    bus_solve = jnp.einsum(
        "tij,tjr->tir", inverse_blocks, net_in, preferred_element_type=jnp.float32
    ).astype(jnp.bfloat16)
    solve_flat = jnp.transpose(bus_solve, (1, 0, 2)).reshape(bus_rows, per_dev * rhs_cols)
    reduced = lax.psum_scatter(
        lax.dot_general(
            sensitivity, solve_flat, (((0,), (0,)), ((), ())), preferred_element_type=jnp.float32
        ),
        "bus",
        scatter_dimension=0,
        tiled=True,
    )
    unit_right = unit_rhs + jnp.transpose(reduced.reshape(unit_rows, per_dev, rhs_cols), (1, 0, 2))
    blocks_count = 1
    block_cols = rhs_cols // blocks_count
    section_count = groups + blocks_count - 1
    costate = jnp.zeros((per_dev, unit_rows, rhs_cols), jnp.float32)
    outgoing = jnp.zeros((unit_rows, block_cols), jnp.float32)
    for section_index in range(section_count):
        incoming = passed_along(outgoing.astype(jnp.bfloat16), "period", -1).astype(outgoing.dtype)
        block_index = section_index - (groups - 1 - period_rank)
        is_valid = (block_index >= 0) & (block_index < blocks_count)
        later = incoming
        for local_step in reversed(range(per_dev)):
            rounded = later.astype(jnp.bfloat16)

            def transposed(row_start, row_count, weights=gain[local_step], vector=rounded):
                return lax.dot_general(
                    weights, vector, (((0,), (0,)), ((), ())), preferred_element_type=jnp.float32
                )

            summed = lax.psum_scatter(
                transposed(jnp.int32(0), unit_rows * lax.axis_size("bus")),
                "bus",
                scatter_dimension=0,
                tiled=True,
            )
            current = unit_right[local_step] + summed
            costate = jnp.where(is_valid, current[None], costate)
            later = current
        outgoing = later
    costate_round = costate.astype(jnp.bfloat16)
    bus_ids = bus_rank * bus_rows + jnp.arange(bus_rows, dtype=jnp.int32)
    placement = (unit_bus[None, :] == bus_ids[:, None]).astype(jnp.bfloat16)
    storage_path = jnp.zeros((per_dev, unit_rows, rhs_cols), jnp.float32)
    bus_update = jnp.zeros((per_dev, bus_rows, rhs_cols), jnp.float32)
    outgoing = jnp.zeros((unit_rows, block_cols), jnp.float32)
    for section_index in range(section_count):
        incoming = passed_along(outgoing.astype(jnp.bfloat16), "period", 1).astype(outgoing.dtype)
        block_index = section_index - period_rank
        is_valid = (block_index >= 0) & (block_index < blocks_count)
        current = jnp.where(period_rank == 0, start_state, incoming)
        local_step = 0
        rounded = current.astype(jnp.bfloat16)
        own_costate = costate_round[local_step]
        whole_state = lax.all_gather(rounded, "bus", axis=0, tiled=True)
        whole_costate = lax.all_gather(own_costate, "bus", axis=0, tiled=True)
        coupling = jnp.dot(schur[local_step], whole_costate, preferred_element_type=jnp.float32)
        injection = jnp.dot(placement, whole_state, preferred_element_type=jnp.float32)
        network = (weighted[local_step] - injection).astype(jnp.bfloat16)
        angle = jnp.dot(inverse_blocks[local_step], network, preferred_element_type=jnp.float32)
        advanced = (
            jnp.dot(gain[local_step], whole_state, preferred_element_type=jnp.float32) - coupling
        )
        storage_path = jnp.where(is_valid, advanced[None], storage_path)
        bus_update = jnp.where(is_valid, angle[None], bus_update)
        current = advanced
        outgoing = current
    return (storage_path, costate, bus_update)


def solution(mesh):
    placed = (
        P("period", "bus", None),
        P("period", "bus", None),
        P("period", "bus", None),
        P("bus", None),
        P("period", "bus", None),
        P("period", "bus", None),
        P("bus", None),
        P("period", "bus"),
        P(),
    )
    return jax.shard_map(
        body,
        mesh=mesh,
        in_specs=placed,
        out_specs=(P("period", "bus", None), P("period", "bus", None), P("period", "bus", None)),
        check_vma=False,
    )
```

profile of v0, /device:TPU:7, one launch (start us, length us, event | category | flops | bytes accessed | tf_op | source)
XLA Modules:
  0.0 1678.6 jit_solution(13985205716786645269)
XLA Ops:
  8.5 4.9 convolution_bitcast_fusion.4
  13.4 5.3 copy.22
  22.3 2.7 convolution_bitcast_fusion.3
  25.0 5.4 copy.24
  30.6 129.5 %reduce-scatter.16.cloned.1.call-done = f32[64,512]{1,0:T(8,128)} async-done(((f32[2048,512]{1,0:T(8,128)}), f32[64,512]{1,0:T(8,128)}) %reduce-scatter.16.cloned.1.call-update) | async-done | bytes 131088 | tf_op jit(solution)/shard_map/reduce_scatter | solution.py:36
  160.0 166.7 %reduce-scatter.18.cloned.1.call-done = f32[64,512]{1,0:T(8,128)} async-done(((f32[2048,512]{1,0:T(8,128)}), f32[64,512]{1,0:T(8,128)}) %reduce-scatter.18.cloned.1.call-update) | async-done | bytes 131088 | tf_op jit(solution)/shard_map/reduce_scatter | solution.py:63
  327.8 25.2 %collective-permute-start.2 = (bf16[64,512]{1,0:T(8,128)(2,1)S(1)}, bf16[64,512]{1,0:T(8,128)(2,1)S(1)}, u32[]{:S(2)}, u32[]{:S(2)}) collective-permute-start(bf16[64,512]{1,0:T(8,128)(2,1)S(1)} %get-tuple-element.11), channel_id=1, source_target_pairs={{32,0},{64,32},{96,64},{33,1},{65,33},{97,65},{34,2},{66,34},{98,6... | collective-permute-start | bytes 196616 | tf_op jit(solution)/shard_map/ppermute | solution.py:10
  353.8 2.8 convolution_bitcast_fusion.2
  356.6 5.3 copy.26
  362.0 143.2 %reduce-scatter.20.cloned.1.call-done = f32[64,512]{1,0:T(8,128)} async-done(((f32[2048,512]{1,0:T(8,128)}), f32[64,512]{1,0:T(8,128)}) %reduce-scatter.20.cloned.1.call-update) | async-done | bytes 131088 | tf_op jit(solution)/shard_map/reduce_scatter | solution.py:63
  506.1 24.8 %collective-permute-start.3 = (bf16[64,512]{1,0:T(8,128)(2,1)S(1)}, bf16[64,512]{1,0:T(8,128)(2,1)S(1)}, u32[]{:S(2)}, u32[]{:S(2)}) collective-permute-start(bf16[64,512]{1,0:T(8,128)(2,1)S(1)} %fusion.92), channel_id=1, source_target_pairs={{32,0},{64,32},{96,64},{33,1},{65,33},{97,65},{34,2},{66,34},{98,6... | collective-permute-start | bytes 196616 | tf_op jit(solution)/shard_map/ppermute | solution.py:10
  531.8 2.8 convolution_bitcast_fusion.1
  534.6 5.3 copy.28
  540.0 142.8 %reduce-scatter.22.cloned.1.call-done = f32[64,512]{1,0:T(8,128)} async-done(((f32[2048,512]{1,0:T(8,128)}), f32[64,512]{1,0:T(8,128)}) %reduce-scatter.22.cloned.1.call-update) | async-done | bytes 131088 | tf_op jit(solution)/shard_map/reduce_scatter | solution.py:63
  683.7 25.8 %collective-permute-start.4 = (bf16[64,512]{1,0:T(8,128)(2,1)S(1)}, bf16[64,512]{1,0:T(8,128)(2,1)S(1)}, u32[]{:S(2)}, u32[]{:S(2)}) collective-permute-start(bf16[64,512]{1,0:T(8,128)(2,1)S(1)} %fusion.93), channel_id=1, source_target_pairs={{32,0},{64,32},{96,64},{33,1},{65,33},{97,65},{34,2},{66,34},{98,6... | collective-permute-start | bytes 196616 | tf_op jit(solution)/shard_map/ppermute | solution.py:10
  710.4 2.8 convolution_bitcast_fusion
  713.1 5.3 copy.30
  718.6 142.7 %reduce-scatter.24.cloned.1.call-done = f32[64,512]{1,0:T(8,128)} async-done(((f32[2048,512]{1,0:T(8,128)}), f32[64,512]{1,0:T(8,128)}) %reduce-scatter.24.cloned.1.call-update) | async-done | bytes 131088 | tf_op jit(solution)/shard_map/reduce_scatter | solution.py:63
  864.3 25.2 %collective-permute-done = bf16[64,512]{1,0:T(8,128)(2,1)S(1)} collective-permute-done((bf16[64,512]{1,0:T(8,128)(2,1)S(1)}, bf16[64,512]{1,0:T(8,128)(2,1)S(1)}, u32[]{:S(2)}, u32[]{:S(2)}) %collective-permute-start) | collective-permute-done | bytes 65568 | tf_op jit(solution)/shard_map/ppermute | solution.py:10
  890.2 126.9 %all-gather.8.cloned.1.call-done = bf16[2048,512]{1,0:T(8,128)(2,1)} async-done(((bf16[64,512]{1,0:T(8,128)(2,1)}), bf16[2048,512]{1,0:T(8,128)(2,1)}) %all-gather.8.cloned.1.call-update) | async-done | bytes 2097168 | tf_op jit(solution)/shard_map/all_gather | solution.py:88
  1019.2 153.2 %all-gather.6.cloned.1.call-done = bf16[2048,512]{1,0:T(8,128)(2,1)} async-done(((bf16[64,512]{1,0:T(8,128)(2,1)}), bf16[2048,512]{1,0:T(8,128)(2,1)}) %all-gather.6.cloned.1.call-update) | async-done | bytes 2097168 | tf_op jit(solution)/shard_map/all_gather | solution.py:87
  1175.8 23.0 %collective-permute-done.5 = bf16[64,512]{1,0:T(8,128)(2,1)S(1)} collective-permute-done((bf16[64,512]{1,0:T(8,128)(2,1)S(1)}, bf16[64,512]{1,0:T(8,128)(2,1)S(1)}, u32[]{:S(2)}, u32[]{:S(2)}) %collective-permute-start.5) | collective-permute-done | bytes 65568 | tf_op jit(solution)/shard_map/ppermute | solution.py:10
  1199.5 135.9 %all-gather.10.cloned.1.call-done = bf16[2048,512]{1,0:T(8,128)(2,1)} async-done(((bf16[64,512]{1,0:T(8,128)(2,1)}), bf16[2048,512]{1,0:T(8,128)(2,1)}) %all-gather.10.cloned.1.call-update) | async-done | bytes 2097168 | tf_op jit(solution)/shard_map/all_gather | solution.py:87
  1339.0 23.0 %collective-permute-done.6 = bf16[64,512]{1,0:T(8,128)(2,1)S(1)} collective-permute-done((bf16[64,512]{1,0:T(8,128)(2,1)S(1)}, bf16[64,512]{1,0:T(8,128)(2,1)S(1)}, u32[]{:S(2)}, u32[]{:S(2)}) %collective-permute-start.6) | collective-permute-done | bytes 65568 | tf_op jit(solution)/shard_map/ppermute | solution.py:10
  1362.8 135.9 %all-gather.12.cloned.1.call-done = bf16[2048,512]{1,0:T(8,128)(2,1)} async-done(((bf16[64,512]{1,0:T(8,128)(2,1)}), bf16[2048,512]{1,0:T(8,128)(2,1)}) %all-gather.12.cloned.1.call-update) | async-done | bytes 2097168 | tf_op jit(solution)/shard_map/all_gather | solution.py:87
  1502.0 23.0 %collective-permute-done.7 = bf16[64,512]{1,0:T(8,128)(2,1)S(1)} collective-permute-done((bf16[64,512]{1,0:T(8,128)(2,1)S(1)}, bf16[64,512]{1,0:T(8,128)(2,1)S(1)}, u32[]{:S(2)}, u32[]{:S(2)}) %collective-permute-start.7) | collective-permute-done | bytes 65568 | tf_op jit(solution)/shard_map/ppermute | solution.py:10
  1525.8 3.7 fusion.51
  1529.5 3.6 fusion.48
  1533.1 128.6 %all-gather.14.cloned.1.call-done = bf16[2048,512]{1,0:T(8,128)(2,1)} async-done(((bf16[64,512]{1,0:T(8,128)(2,1)}), bf16[2048,512]{1,0:T(8,128)(2,1)}) %all-gather.14.cloned.1.call-update) | async-done | bytes 2097168 | tf_op jit(solution)/shard_map/all_gather | solution.py:87
  1661.7 3.6 fusion.45
  1665.3 2.7 fusion.54
  1668.0 3.7 fusion.31
  (69 shorter events, 28.7 us)
Async XLA Ops:
  7.2 1.3 copy-start
  7.2 152.9 %reduce-scatter.16.cloned.1.call-start = ((), (), s32[]{:S(2)}) async-start(), calls=%async_computation.10 | async-start | bytes 4325376 | tf_op jit(solution)/shard_map/reduce_scatter | solution.py:36
  18.7 3.6 copy-start.1
  18.8 308.0 %reduce-scatter.18.cloned.1.call-start = ((), (), s32[]{:S(2)}) async-start(), calls=%async_computation.11 | async-start | bytes 4325376 | tf_op jit(solution)/shard_map/reduce_scatter | solution.py:63
  18.8 3.5 collective-permute-start.1
  30.5 296.3 %copy-start.9 = (f32[1,64,512]{2,1,0:T(8,128)S(1)}, f32[1,64,512]{2,1,0:T(8,128)}, u32[]{:S(2)}) copy-start(f32[1,64,512]{2,1,0:T(8,128)} %param.14) | copy-start | bytes 393220
  30.5 474.7 %reduce-scatter.20.cloned.1.call-start = ((), (), s32[]{:S(2)}) async-start(), calls=%async_computation.12 | async-start | bytes 4325376 | tf_op jit(solution)/shard_map/reduce_scatter | solution.py:63
  327.8 26.1 %collective-permute-start.2 = (bf16[64,512]{1,0:T(8,128)(2,1)S(1)}, bf16[64,512]{1,0:T(8,128)(2,1)S(1)}, u32[]{:S(2)}, u32[]{:S(2)}) collective-permute-start(bf16[64,512]{1,0:T(8,128)(2,1)S(1)} %get-tuple-element.11), channel_id=1, source_target_pairs={{32,0},{64,32},{96,64},{33,1},{65,33},{97,65},{34,2},{66,34},{98,6... | collective-permute-start | bytes 196616 | tf_op jit(solution)/shard_map/ppermute | solution.py:10
  362.0 320.8 %reduce-scatter.22.cloned.1.call-start = ((), (), s32[]{:S(2)}) async-start(), calls=%async_computation.13 | async-start | bytes 4325376 | tf_op jit(solution)/shard_map/reduce_scatter | solution.py:63
  506.1 25.7 %collective-permute-start.3 = (bf16[64,512]{1,0:T(8,128)(2,1)S(1)}, bf16[64,512]{1,0:T(8,128)(2,1)S(1)}, u32[]{:S(2)}, u32[]{:S(2)}) collective-permute-start(bf16[64,512]{1,0:T(8,128)(2,1)S(1)} %fusion.92), channel_id=1, source_target_pairs={{32,0},{64,32},{96,64},{33,1},{65,33},{97,65},{34,2},{66,34},{98,6... | collective-permute-start | bytes 196616 | tf_op jit(solution)/shard_map/ppermute | solution.py:10
  539.9 321.4 %reduce-scatter.24.cloned.1.call-start = ((), (), s32[]{:S(2)}) async-start(), calls=%async_computation.14 | async-start | bytes 4325376 | tf_op jit(solution)/shard_map/reduce_scatter | solution.py:63
  683.7 26.7 %collective-permute-start.4 = (bf16[64,512]{1,0:T(8,128)(2,1)S(1)}, bf16[64,512]{1,0:T(8,128)(2,1)S(1)}, u32[]{:S(2)}, u32[]{:S(2)}) collective-permute-start(bf16[64,512]{1,0:T(8,128)(2,1)S(1)} %fusion.93), channel_id=1, source_target_pairs={{32,0},{64,32},{96,64},{33,1},{65,33},{97,65},{34,2},{66,34},{98,6... | collective-permute-start | bytes 196616 | tf_op jit(solution)/shard_map/ppermute | solution.py:10
  718.5 142.8 %copy-start.4 = (f32[64,512]{1,0:T(8,128)S(1)}, f32[64,512]{1,0:T(8,128)}, u32[]{:S(2)}) copy-start(f32[64,512]{1,0:T(8,128)} %reduce-scatter.20.cloned.1.call-done) | copy-start | bytes 393220
  718.5 142.8 %copy-start.5 = (f32[64,512]{1,0:T(8,128)S(1)}, f32[64,512]{1,0:T(8,128)}, u32[]{:S(2)}) copy-start(f32[64,512]{1,0:T(8,128)} %reduce-scatter.22.cloned.1.call-done) | copy-start | bytes 393220
  718.5 142.8 %copy-start.6 = (f32[64,512]{1,0:T(8,128)S(1)}, f32[64,512]{1,0:T(8,128)}, u32[]{:S(2)}) copy-start(f32[64,512]{1,0:T(8,128)} %reduce-scatter.18.cloned.1.call-done) | copy-start | bytes 393220
  718.5 171.0 %copy-start.2 = (f32[64,512]{1,0:T(8,128)S(1)}, f32[64,512]{1,0:T(8,128)}, u32[]{:S(2)}) copy-start(f32[64,512]{1,0:T(8,128)} %param.15) | copy-start | bytes 393220
  718.5 298.6 %copy-start.7 = (bf16[1,64,2048]{2,1,0:T(8,128)(2,1)S(1)}, bf16[1,64,2048]{2,1,0:T(8,128)(2,1)}, u32[]{:S(2)}) copy-start(bf16[1,64,2048]{2,1,0:T(8,128)(2,1)} %param.10) | copy-start | bytes 786436
  718.5 298.6 %all-gather.8.cloned.1.call-start = ((), (), s32[]{:S(2)}) async-start(), calls=%async_computation.6 | async-start | bytes 2162688 | tf_op jit(solution)/shard_map/all_gather | solution.py:88
  863.0 309.4 %all-gather.6.cloned.1.call-start = ((), (), s32[]{:S(2)}) async-start(), calls=%async_computation.5 | async-start | bytes 2162688 | tf_op jit(solution)/shard_map/all_gather | solution.py:87
  863.0 26.5 %collective-permute-start = (bf16[64,512]{1,0:T(8,128)(2,1)S(1)}, bf16[64,512]{1,0:T(8,128)(2,1)S(1)}, u32[]{:S(2)}, u32[]{:S(2)}) collective-permute-start(bf16[64,512]{1,0:T(8,128)(2,1)S(1)} %broadcast.61), channel_id=1, source_target_pairs={{0,32},{32,64},{64,96},{1,33},{33,65},{65,97},{2,34},{34,66},{66,9... | collective-permute-start | bytes 196616 | tf_op jit(solution)/shard_map/ppermute | solution.py:10
  890.2 445.3 %all-gather.10.cloned.1.call-start = ((), (), s32[]{:S(2)}) async-start(), calls=%async_computation.7 | async-start | bytes 2162688 | tf_op jit(solution)/shard_map/all_gather | solution.py:87
  1174.5 24.3 %collective-permute-start.5 = (bf16[64,512]{1,0:T(8,128)(2,1)S(1)}, bf16[64,512]{1,0:T(8,128)(2,1)S(1)}, u32[]{:S(2)}, u32[]{:S(2)}) collective-permute-start(bf16[64,512]{1,0:T(8,128)(2,1)S(1)} %convert_bitcast_fusion.2), channel_id=1, source_target_pairs={{0,32},{32,64},{64,96},{1,33},{33,65},{65,97},{2,34},{34,66},{66,9... | collective-permute-start | bytes 196616 | tf_op jit(solution)/shard_map/ppermute | solution.py:10
  1199.5 299.2 %all-gather.12.cloned.1.call-start = ((), (), s32[]{:S(2)}) async-start(), calls=%async_computation.8 | async-start | bytes 2162688 | tf_op jit(solution)/shard_map/all_gather | solution.py:87
  1337.5 188.3 %copy-start.3 = (f32[1,320,512]{2,1,0:T(8,128)S(1)}, f32[1,320,512]{2,1,0:T(8,128)}, u32[]{:S(2)}) copy-start(f32[1,320,512]{2,1,0:T(8,128)} %param.13) | copy-start | bytes 1966084
  1337.5 188.3 %copy-start.8 = (bf16[1,320,320]{2,1,0:T(8,128)(2,1)S(1)}, bf16[1,320,320]{2,1,0:T(8,128)(2,1)}, u32[]{:S(2)}) copy-start(bf16[1,320,320]{2,1,0:T(8,128)(2,1)} %param.11) | copy-start | bytes 614404
  1337.5 188.3 %copy-start.10 = (s32[2048]{0:T(1024)S(1)}, s32[2048]{0:T(1024)}, u32[]{:S(2)}) copy-start(s32[2048]{0:T(1024)} %param.17) | copy-start | bytes 24580
  1337.6 24.5 %collective-permute-start.6 = (bf16[64,512]{1,0:T(8,128)(2,1)S(1)}, bf16[64,512]{1,0:T(8,128)(2,1)S(1)}, u32[]{:S(2)}, u32[]{:S(2)}) collective-permute-start(bf16[64,512]{1,0:T(8,128)(2,1)S(1)} %convert_bitcast_fusion.1), channel_id=1, source_target_pairs={{0,32},{32,64},{64,96},{1,33},{33,65},{65,97},{2,34},{34,66},{66,9... | collective-permute-start | bytes 196616 | tf_op jit(solution)/shard_map/ppermute | solution.py:10
  1362.7 299.0 %all-gather.14.cloned.1.call-start = ((), (), s32[]{:S(2)}) async-start(), calls=%async_computation.9 | async-start | bytes 2162688 | tf_op jit(solution)/shard_map/all_gather | solution.py:87
  1500.7 24.3 %collective-permute-start.7 = (bf16[64,512]{1,0:T(8,128)(2,1)S(1)}, bf16[64,512]{1,0:T(8,128)(2,1)S(1)}, u32[]{:S(2)}, u32[]{:S(2)}) collective-permute-start(bf16[64,512]{1,0:T(8,128)(2,1)S(1)} %convert_bitcast_fusion), channel_id=1, source_target_pairs={{0,32},{32,64},{64,96},{1,33},{33,65},{65,97},{2,34},{34,66},{66,9... | collective-permute-start | bytes 196616 | tf_op jit(solution)/shard_map/ppermute | solution.py:10
Sparse Core Ops, SparseCore 0:
  18.9 141.1 reduce-scatter.15
  162.4 164.3 reduce-scatter.17
  362.1 143.0 reduce-scatter.19
  540.1 142.6 reduce-scatter.21
  718.6 142.6 reduce-scatter.23
  863.4 153.7 all-gather.7
  1019.3 153.0 all-gather.5
  1199.6 135.7 all-gather.9
  1362.8 135.7 all-gather.11
  1525.9 135.7 all-gather.13
where the time goes:
time: 1710 us; the launch traced here: 1680 us
  waiting for transfers between devices  1500 us (88%)
  starting transfers between devices  84.1 us (5%)
  matrix products  41.5 us (2%)
  local copies, waits for them, and re-layouts  27.3 us (2%)
    reduce_scatter x4, waiting for transfers between devices, body(): lax.psum_scatter(transposed(jnp.int32(0), unit_rows * lax.axis_size('bus'...  595 us
    all_gather x4, waiting for transfers between devices, body(): whole_state = lax.all_gather(rounded, 'bus', axis=0, tiled=True)  554 us
    reduce_scatter x1, waiting for transfers between devices, body(): lax.psum_scatter(lax.dot_general(sensitivity, solve_flat, (((0,), (0,)),...  129 us
    all_gather x1, waiting for transfers between devices, body(): whole_costate = lax.all_gather(own_costate, 'bus', axis=0, tiled=True)  127 us
    ppermute x8, waiting for transfers between devices, passed_along(): return lax.ppermute(block, axis, route)  97.8 us
    ppermute x8, starting transfers between devices, passed_along(): return lax.ppermute(block, axis, route)  83.7 us
  transfers between devices with their start and end apart: 18, of which 18 were waited for; matrix products, arithmetic and copies ran while one was open for 1% of the time, Pallas kernels for 0%

commit v1 on v0

v1 whole, which is shorter than its diff:
```python
import jax
import jax.numpy as jnp
from jax import lax
from jax.experimental import pallas as pl
from jax.experimental.pallas import tpu as pltpu
from jax.sharding import PartitionSpec as P

MESH = pl.DeviceIdType.MESH
T = 4
X = 4
S = 16
F32 = jnp.float32
BF16 = jnp.bfloat16


def dot(a, b):
    return jnp.dot(a, b, preferred_element_type=F32)


def kernel(
    gain, schur, inverse, sens, resid, rhs, start, active, unit_bus,
    stor_out, cost_out, upd_out,
    sens_half, sens_t, resid_v, inv_v, act_v, ubus_v, start_v, start_b, weighted_v, solve_s, solve_r,
    gain_s, schur_s, gain_r, schur_r, gain_t, rhs_r, part_v, rs_s, rs_r, cost_v, cost_g, cost_p,
    state_v, state_g, full_v, full_r, onehot, inj_s, inj_r, upd_v,
    load_sem, sens_sem, solve_sem, gain_sem, schur_sem, rhs_sem, first_sem, rs_sem, cg_sem, xg_sem, pair_sem, full_sem,
    inj_sem, cout_sem, sout_sem, send_ring, send_plane,
):
    period = lax.axis_index("period")
    bus = lax.axis_index("bus")
    x_hi, core = lax.div(period, 2), lax.rem(period, 2)
    z, x_lo, y = lax.div(bus, 8), lax.rem(lax.div(bus, 4), 2), lax.rem(bus, 4)
    x = 2 * x_hi + x_lo
    spot = z * 4 + y
    x_pair = x + 1 - 2 * x_lo
    cols = 128

    def ring_id(xx, kk):
        return (2 * lax.div(xx, 2) + kk, z * 8 + lax.rem(xx, 2) * 4 + y)

    def plane_id(ss):
        return (period, lax.div(ss, 4) * 8 + x_lo * 4 + lax.rem(ss, 4))

    def lanes(xx):
        return pl.ds(pl.multiple_of(xx * cols, cols), cols)

    sent = []

    def ring_copy(src, dst, recv, xx, kk):
        send = send_ring.at[len(sent)]
        mine = (x == xx) & (core == kk)
        remote = pltpu.make_async_remote_copy(
            src_ref=src, dst_ref=dst, send_sem=send, recv_sem=recv, device_id=ring_id(xx, kk), device_id_type=MESH
        )

        @pl.when(mine)
        def _():
            pltpu.make_async_copy(src, dst, recv).start()

        @pl.when(jnp.logical_not(mine))
        def _():
            remote.start()

        sent.append((jnp.logical_not(mine), remote))

    def far_copy(src, dst, recv, xx, kk, on=None):
        send = send_ring.at[len(sent)]
        remote = pltpu.make_async_remote_copy(
            src_ref=src, dst_ref=dst, send_sem=send, recv_sem=recv, device_id=ring_id(xx, kk), device_id_type=MESH
        )
        if on is None:
            remote.start()
        else:
            pl.when(on)(remote.start)
        sent.append((on, remote))

    plane_sent = []

    def plane_copy(src_at, dst, recv):
        send = send_plane.at[len(plane_sent)]

        def one(i, carry):
            ss = lax.rem(spot + i, S)
            pltpu.make_async_remote_copy(
                src_ref=src_at(ss), dst_ref=dst, send_sem=send, recv_sem=recv, device_id=plane_id(ss), device_id_type=MESH
            ).start()
            return carry

        lax.fori_loop(1, S, one, 0)
        plane_sent.append(send)

    def plane_wait(buf, sem):
        some = buf.at[pl.ds(0, S - 1)]
        pltpu.make_async_copy(some, some, sem).wait()

    def landed(ref, sem):
        pltpu.make_async_copy(ref, ref, sem).wait()

    barrier = pltpu.get_barrier_semaphore()
    for i in range(1, 8):
        there = lax.rem(x * 2 + core + i, 8)
        pl.semaphore_signal(
            barrier, inc=1, device_id=ring_id(lax.div(there, 2), lax.rem(there, 2)), device_id_type=MESH
        )

    def greet(i, carry):
        pl.semaphore_signal(barrier, inc=1, device_id=plane_id(lax.rem(spot + i, S)), device_id_type=MESH)
        return carry

    lax.fori_loop(1, S, greet, 0)

    for i in range(4):
        strip = pl.ds(pl.multiple_of(i * 512 + core * 256, 256), 256)
        pltpu.make_async_copy(sens.at[:, strip], sens_half.at[x_lo, :, pl.ds(i * 256, 256)], load_sem.at[0]).start()
    load_resid = pltpu.make_async_copy(resid.at[0], resid_v, load_sem.at[1])
    load_inv = pltpu.make_async_copy(inverse.at[0], inv_v, load_sem.at[2])
    load_act = pltpu.make_async_copy(active, act_v, load_sem.at[3])
    load_start = pltpu.make_async_copy(start, start_v, load_sem.at[4])
    load_ubus = pltpu.make_async_copy(unit_bus, ubus_v, load_sem.at[5])
    for load in (load_resid, load_inv, load_act, load_start, load_ubus):
        load.start()
    for source, stage, sem in ((gain, gain_s, load_sem.at[6]), (schur, schur_s, load_sem.at[7])):
        for kk in range(2):
            for i in range(4):
                pltpu.make_async_copy(
                    source.at[0, :, pl.ds(i * 512 + kk * 256, 256)], stage.at[kk, :, pl.ds(i * 256, 256)], sem
                ).start()

    landed(sens_half.at[x_lo], load_sem.at[0])
    pl.semaphore_wait(barrier, 22)

    half = sens_half.shape[1] // 2
    for i, step in enumerate((1, X - 1)):
        rows = pl.ds(i * half, half)
        far_copy(
            sens_half.at[x_lo, rows], sens_half.at[x_lo, rows], sens_sem.at[i], lax.rem(x + step, X), core
        )

    load_resid.wait()
    load_inv.wait()
    load_act.wait()
    n = inv_v.shape[0]
    diagonal = lax.broadcasted_iota(jnp.int32, (n, n), 0) == lax.broadcasted_iota(jnp.int32, (n, n), 1)
    scale = 1.0 + 3.0 * act_v[...].astype(F32)
    scale = jnp.sum(jnp.where(diagonal, jnp.broadcast_to(scale, (n, n)), 0.0), axis=1, keepdims=True)
    weighted = resid_v[...] * scale
    weighted_v[...] = weighted
    solve_s[...] = dot(inv_v[...], weighted.astype(BF16)).astype(BF16)
    for xx in (0, 1, 2, 3):
        for kk in (0, 1):
            ring_copy(
                solve_s.at[:, lanes(xx)], solve_r.at[x_lo, :, lanes(period)], solve_sem.at[period * 2 + x_lo], xx, kk
            )

    load_start.wait()
    start_b[...] = start_v[...].astype(BF16)
    own = x_lo == core

    @pl.when(own)
    def _():
        state_g[0, spot] = start_b[:, lanes(x)]

    far_copy(start_b.at[:, lanes(x_pair)], state_g.at[0, spot], first_sem.at[0], x_pair, core, own)

    for xx in range(X):
        ring_copy(rhs.at[0, :, lanes(xx)], rhs_r.at[period], rhs_sem.at[period], xx, x_lo)

    landed(gain_s, load_sem.at[6])
    for xx in range(X):
        for kk in range(2):
            ring_copy(gain_s.at[kk], gain_r.at[period, x_lo], gain_sem.at[period * 2 + x_lo], xx, kk)

    @pl.when(jnp.logical_not(own))
    def _():
        landed(state_g.at[0, spot], first_sem.at[0])

    plane_copy(lambda ss: state_g.at[0, spot], state_g.at[0, spot], xg_sem.at[0])

    landed(schur_s, load_sem.at[7])
    for xx in range(X):
        for kk in range(2):
            ring_copy(schur_s.at[kk], schur_r.at[period, x_lo], schur_sem.at[period * 2 + x_lo], xx, kk)

    load_ubus.wait()
    for i in range(4):
        units = ubus_v[:, pl.ds(pl.multiple_of(i * 512 + core * 256, 256), 256)]
        for j in range(2):
            first = (z * 8 + j * 4 + y) * n
            ids = lax.broadcasted_iota(jnp.int32, (n, 256), 0) + first
            onehot[j * n : (j + 1) * n, i * 256 : (i + 1) * 256] = jnp.where(
                ids == jnp.broadcast_to(units, (n, 256)), 1.0, 0.0
            ).astype(BF16)

    for i in range(2):
        rows = pl.ds(i * half, half)
        landed(sens_half.at[1 - x_lo, rows], sens_sem.at[i])
    for j in range(2):
        sens_t[j] = sens_half[j].T
    for t in range(T):
        for j in range(2):
            landed(solve_r.at[j, :, lanes(t)], solve_sem.at[t * 2 + j])

    def reduce_start(t, partial):
        rs_s[t] = partial.astype(BF16).reshape(S, 64, cols)
        plane_copy(lambda ss: rs_s.at[t, ss], rs_r.at[t, spot], rs_sem.at[t])
        rs_r[t, spot] = rs_s[t, spot]

    last = (T - 1) * cols
    reduce_start(T - 1, dot(sens_t[0], solve_r[0, :, last:]) + dot(sens_t[1], solve_r[1, :, last:]))
    part_v[...] = dot(sens_t[0], solve_r[0, :, :last]) + dot(sens_t[1], solve_r[1, :, :last])

    for t in reversed(range(T)):
        if t < T - 1:
            for j in range(2):
                landed(gain_r.at[t, j], gain_sem.at[t * 2 + j])
                gain_t[t, :, j * 64 : (j + 1) * 64] = gain_r[t, j].T
            landed(cost_p.at[t + 1, 1 - core], pair_sem.at[t + 1])
            reduce_start(
                t, part_v[:, t * cols : (t + 1) * cols] + dot(gain_t[t], cost_p[t + 1].reshape(2 * 64, cols))
            )
            plane_copy(lambda ss, t=t: cost_g.at[t + 1, spot], cost_g.at[t + 1, spot], cg_sem.at[t + 1])
        landed(rhs_r.at[t], rhs_sem.at[t])
        plane_wait(rs_r.at[t], rs_sem.at[t])
        total = rhs_r[t] + jnp.sum(rs_r[t].astype(F32), axis=0)
        cost_v[t] = total
        rounded = total.astype(BF16)
        cost_g[t, spot] = rounded
        if t > 0:
            cost_p[t, core] = rounded
            far_copy(cost_g.at[t, spot], cost_p.at[t, core], pair_sem.at[t], x, 1 - core)
        else:
            plane_copy(lambda ss: cost_g.at[0, spot], cost_g.at[0, spot], cg_sem.at[0])
        ring_copy(cost_v.at[t], cost_out.at[0, :, lanes(x)], cout_sem.at[x], 2 * (t // 2) + core, t % 2)

    for t in range(T):
        for j in range(2):
            if t == T - 1:
                landed(gain_r.at[t, j], gain_sem.at[t * 2 + j])
            landed(schur_r.at[t, j], schur_sem.at[t * 2 + j])
        width = S * 64
        plane_wait(state_g.at[t], xg_sem.at[t])
        if t == T - 1:
            moved = dot(onehot[...], state_g[t].reshape(width, cols))
            inj_s[t] = moved.astype(BF16).reshape(2, n, cols)
            for j in range(2):
                ring_copy(
                    inj_s.at[t, j], inj_r.at[core, :, lanes(x)], inj_sem.at[x * 2 + core], 2 * (t // 2) + j, t % 2
                )
        plane_wait(cost_g.at[t], cg_sem.at[t])
        full = dot(gain_r[t].reshape(2 * 64, width), state_g[t].reshape(width, cols)) - dot(
            schur_r[t].reshape(2 * 64, width), cost_g[t].reshape(width, cols)
        )
        full_v[t] = full.reshape(2, 64, cols)
        far_copy(full_v.at[t, 1 - core], full_r.at[t], full_sem.at[t], x, 1 - core)
        if t < T - 1:
            moved = dot(onehot[...], state_g[t].reshape(width, cols))
            inj_s[t] = moved.astype(BF16).reshape(2, n, cols)
        landed(full_r.at[t], full_sem.at[t])
        total = full_v[t, core] + full_r[t]
        state_v[t] = total
        if t < T - 1:
            state_g[t + 1, spot] = total.astype(BF16)
            plane_copy(lambda ss, t=t: state_g.at[t + 1, spot], state_g.at[t + 1, spot], xg_sem.at[t + 1])
        ring_copy(state_v.at[t], stor_out.at[0, :, lanes(x)], sout_sem.at[x], 2 * (t // 2) + core, t % 2)
        if t < T - 1:
            for j in range(2):
                ring_copy(
                    inj_s.at[t, j], inj_r.at[core, :, lanes(x)], inj_sem.at[x * 2 + core], 2 * (t // 2) + j, t % 2
                )

    for xx in range(X):
        for kk in range(2):
            landed(inj_r.at[kk, :, lanes(xx)], inj_sem.at[xx * 2 + kk])
    network = weighted_v[...] - (inj_r[0].astype(F32) + inj_r[1].astype(F32))
    upd_v[...] = dot(inv_v[...], network.astype(BF16))
    store = pltpu.make_async_copy(upd_v, upd_out.at[0], load_sem.at[8])
    store.start()
    for xx in range(X):
        landed(cost_out.at[0, :, lanes(xx)], cout_sem.at[xx])
        landed(stor_out.at[0, :, lanes(xx)], sout_sem.at[xx])
    for on, copy in sent:
        if on is None:
            copy.wait_send()
        else:
            pl.when(on)(copy.wait_send)
    for send in plane_sent:
        plane_wait(rs_s.at[0], send)
    store.wait()


def body(gain, schur, inverse_blocks, sensitivity, residual_bus, unit_rhs, start_state, active_set, unit_bus):
    anywhere = pl.BlockSpec(memory_space=pl.ANY)
    n = inverse_blocks.shape[1]
    dma = pltpu.SemaphoreType.DMA
    scratch = [
        pltpu.VMEM((2, n, 1024), BF16),
        pltpu.VMEM((2, 1024, n), BF16),
        pltpu.VMEM((n, 512), F32),
        pltpu.VMEM((n, n), BF16),
        pltpu.VMEM((1, n), jnp.int32),
        pltpu.VMEM((1, 2048), jnp.int32),
        pltpu.VMEM((64, 512), F32),
        pltpu.VMEM((64, 512), BF16),
        pltpu.VMEM((n, 512), F32),
        pltpu.VMEM((n, 512), BF16),
        pltpu.VMEM((2, n, 512), BF16),
        pltpu.VMEM((2, 64, 1024), BF16),
        pltpu.VMEM((2, 64, 1024), BF16),
        pltpu.VMEM((T, 2, 64, 1024), BF16),
        pltpu.VMEM((T, 2, 64, 1024), BF16),
        pltpu.VMEM((T - 1, 1024, 128), BF16),
        pltpu.VMEM((T, 64, 128), F32),
        pltpu.VMEM((1024, 384), F32),
        pltpu.VMEM((T, S, 64, 128), BF16),
        pltpu.VMEM((T, S, 64, 128), BF16),
        pltpu.VMEM((T, 64, 128), F32),
        pltpu.VMEM((T, S, 64, 128), BF16),
        pltpu.VMEM((T, 2, 64, 128), BF16),
        pltpu.VMEM((T, 64, 128), F32),
        pltpu.VMEM((T, S, 64, 128), BF16),
        pltpu.VMEM((T, 2, 64, 128), F32),
        pltpu.VMEM((T, 64, 128), F32),
        pltpu.VMEM((2 * n, 1024), BF16),
        pltpu.VMEM((T, 2, n, 128), BF16),
        pltpu.VMEM((2, n, 512), BF16),
        pltpu.VMEM((n, 512), F32),
        dma((9,)),
        dma((2,)),
        dma((8,)),
        dma((8,)),
        dma((8,)),
        dma((4,)),
        dma((1,)),
        dma((4,)),
        dma((4,)),
        dma((4,)),
        dma((4,)),
        dma((4,)),
        dma((8,)),
        dma((4,)),
        dma((4,)),
        dma((64,)),
        dma((12,)),
    ]
    return pl.pallas_call(
        kernel,
        out_shape=(
            jax.ShapeDtypeStruct((1, 64, 512), F32),
            jax.ShapeDtypeStruct((1, 64, 512), F32),
            jax.ShapeDtypeStruct((1, n, 512), F32),
        ),
        in_specs=[anywhere] * 9,
        out_specs=(anywhere,) * 3,
        scratch_shapes=scratch,
        compiler_params=pltpu.CompilerParams(
            collective_id=0, has_side_effects=True, vmem_limit_bytes=48 * 1024 * 1024
        ),
    )(
        gain, schur, inverse_blocks, sensitivity, residual_bus, unit_rhs, start_state, active_set,
        unit_bus.reshape(1, -1),
    )


def solution(mesh):
    placed = (
        P("period", "bus", None),
        P("period", "bus", None),
        P("period", "bus", None),
        P("bus", None),
        P("period", "bus", None),
        P("period", "bus", None),
        P("bus", None),
        P("period", "bus"),
        P(),
    )
    return jax.shard_map(
        body,
        mesh=mesh,
        in_specs=placed,
        out_specs=(P("period", "bus", None), P("period", "bus", None), P("period", "bus", None)),
        check_vma=False,
    )
```

time: 1710 us -> 111 us (0.06); the launches traced: 1680 us -> 111 us
  waiting for transfers between devices: 1500 us -> 0 us
  Pallas kernels: 0 us -> 99.8 us
  starting transfers between devices: 84.1 us -> 0 us
  matrix products: 41.5 us -> 0 us
    reduce_scatter x5 -> x0, waiting for transfers between devices: 725 us -> none  [the longest x4 595 us: body(): lax.psum_scatter(transposed(jnp.int32(0), unit_rows * lax.axis_size('bus'...]
    all_gather x5 -> x0, waiting for transfers between devices: 681 us -> none  [the longest x4 554 us: body(): whole_state = lax.all_gather(rounded, 'bus', axis=0, tiled=True)]
    pallas_call x0 -> x1, Pallas kernels: none -> 99.8 us  [body(): pl.pallas_call(kernel, out_shape=(jax.ShapeDtypeStruct((1, 64, 512), F32)...]
    ppermute x8 -> x0, waiting for transfers between devices: 97.8 us -> none  [passed_along(): return lax.ppermute(block, axis, route)]
    ppermute x8 -> x0, starting transfers between devices: 83.7 us -> none  [passed_along(): return lax.ppermute(block, axis, route)]
    dot_general x14 -> x0, matrix products: 41.5 us -> none  [the longest x4 14.6 us: body(): jnp.dot(inverse_blocks[local_step], network, preferred_element_type=jnp.f...]
  transfers between devices with their start and end apart: 18 -> 0, of which waited for: 18 -> 0; matrix products, arithmetic and copies ran while one was open for 1% -> 0% of each run, Pallas kernels for 0% -> 0%
where the time goes in v1:
time: 111 us
  Pallas kernels  99.8 us (90%)
  local copies, waits for them, and re-layouts  10.6 us (10%)
    pallas_call x1, Pallas kernels, body(): pl.pallas_call(kernel, out_shape=(jax.ShapeDtypeStruct((1, 64, 512), F32)...  99.8 us
    unnamed x21, local copies, waits for them, and re-layouts  10.6 us

profile of v1, /device:TPU:7, one launch (start us, length us, event | category | flops | bytes accessed | tf_op | source)
XLA Modules:
  0.0 111.0 jit_solution(8796389824074652701)
XLA Ops:
  0.6 0.0 copy-start
  0.6 1.3 %copy-done = bf16[320,2048]{1,0:T(8,128)(2,1)S(1)} copy-done((bf16[320,2048]{1,0:T(8,128)(2,1)S(1)}, bf16[320,2048]{1,0:T(8,128)(2,1)}, u32[]{:S(2)}) %copy-start) | copy-done | bytes 1310744
  2.0 0.0 copy-start.1
  2.0 1.1 copy-done.1
  3.0 0.0 copy-start.2
  3.0 0.9 copy-done.2
  4.0 0.0 copy-start.3
  4.0 0.9 copy-done.3
  4.9 0.0 copy-start.4
  4.9 0.9 copy-done.4
  5.9 0.0 copy-start.5
  5.9 0.9 copy-done.5
  6.8 0.0 copy-start.6
  6.8 0.9 copy-done.6
  7.7 0.0 copy-start.7
  7.7 0.7 copy-done.7
  8.4 0.0 copy-start.8
  8.4 0.7 copy-done.8
  9.1 99.8 %shard_map.112 = (f32[1,64,512]{2,1,0:T(8,128)S(1)}, f32[1,64,512]{2,1,0:T(8,128)S(1)}, f32[1,320,512]{2,1,0:T(8,128)S(1)}) custom-call(bf16[1,64,2048]{2,1,0:T(8,128)(2,1)S(1)} %copy-done.2, bf16[1,64,2048]{2,1,0:T(8,128)(2,1)S(1)} %copy-done.3, bf16[1,320,320]{2,1,0:T(8,128)(2,1)S(1)} %copy-done.4, bf16[320,2048]{1,0:T(8,128)(2,1)S(1)} %copy-done, ...), custom_call_target="tpu_custom_call" | custom-call | tf_op jit(solution)/shard_map/pallas_call | solution.py:345
  108.9 0.7 copy.15
  109.6 0.7 copy.16
  110.2 0.8 copy.17
Async XLA Ops:
  0.6 1.3 %copy-start = (bf16[320,2048]{1,0:T(8,128)(2,1)S(1)}, bf16[320,2048]{1,0:T(8,128)(2,1)}, u32[]{:S(2)}) copy-start(bf16[320,2048]{1,0:T(8,128)(2,1)} %sens.1) | copy-start | bytes 3932164
  2.0 1.1 copy-start.1
  3.0 0.9 copy-start.2
  4.0 0.9 copy-start.3
  4.9 0.9 copy-start.4
  5.9 0.9 copy-start.5
  6.8 0.9 copy-start.6
  7.7 0.7 copy-start.7
  8.4 0.7 copy-start.8

commit v2 on v1

--- a/solution.py
+++ b/solution.py
@@ -44,6 +44,8 @@
     def lanes(xx):
         return pl.ds(pl.multiple_of(xx * cols, cols), cols)
 
+    pend = {}
+    started = set()
     sent = []
 
     def ring_copy(src, dst, recv, xx, kk):
@@ -62,6 +64,34 @@
             remote.start()
 
         sent.append((jnp.logical_not(mine), remote))
+
+    def ring_group(name, copies):
+        made = []
+        for src, dst, recv, xx, kk in copies:
+            mine = (x == xx) & (core == kk)
+            remote = pltpu.make_async_remote_copy(
+                src_ref=src, dst_ref=dst, send_sem=send_ring.at[len(sent)], recv_sem=recv,
+                device_id=ring_id(xx, kk), device_id_type=MESH,
+            )
+            made.append((mine, remote, pltpu.make_async_copy(src, dst, recv)))
+            sent.append([jnp.logical_not(mine), remote, []])
+        mark = sent[-len(made):]
+
+        def start(*periods):
+            for m in mark:
+                m[2].extend(periods)
+            for p in periods:
+                started.add((name, p))
+            on = period == periods[0]
+            for p in periods[1:]:
+                on = on | (period == p)
+            @pl.when(on)
+            def _():
+                for mine, remote, local in made:
+                    pl.when(mine)(local.start)
+                    pl.when(jnp.logical_not(mine))(remote.start)
+
+        return start
 
     def far_copy(src, dst, recv, xx, kk, on=None):
         send = send_ring.at[len(sent)]
@@ -95,6 +125,20 @@
 
     def landed(ref, sem):
         pltpu.make_async_copy(ref, ref, sem).wait()
+
+    def take(key):
+        pend.pop(key)()
+
+    def home_wait(t, fn0):
+        def fn():
+            fn0()
+
+        pl.when(period == t)(fn)
+
+    def inj_wait():
+        for xx in range(X):
+            for kk in range(2):
+                landed(inj_r.at[kk, :, lanes(xx)], inj_sem.at[xx * 2 + kk])
 
     barrier = pltpu.get_barrier_semaphore()
     for i in range(1, 8):
@@ -126,19 +170,16 @@
                     source.at[0, :, pl.ds(i * 512 + kk * 256, 256)], stage.at[kk, :, pl.ds(i * 256, 256)], sem
                 ).start()
 
-    landed(sens_half.at[x_lo], load_sem.at[0])
-    pl.semaphore_wait(barrier, 22)
-
-    half = sens_half.shape[1] // 2
-    for i, step in enumerate((1, X - 1)):
-        rows = pl.ds(i * half, half)
-        far_copy(
-            sens_half.at[x_lo, rows], sens_half.at[x_lo, rows], sens_sem.at[i], lax.rem(x + step, X), core
-        )
-
-    load_resid.wait()
-    load_inv.wait()
-    load_act.wait()
+    pend['load_resid'] = load_resid.wait
+    pend['load_inv'] = load_inv.wait
+    pend['load_act'] = load_act.wait
+    pend['load_start'] = load_start.wait
+    pend['load_ubus'] = load_ubus.wait
+    pend['gain_s'] = lambda: landed(gain_s, load_sem.at[6])
+    pend['schur_s'] = lambda: landed(schur_s, load_sem.at[7])
+    take('load_resid')
+    take('load_inv')
+    take('load_act')
     n = inv_v.shape[0]
     diagonal = lax.broadcasted_iota(jnp.int32, (n, n), 0) == lax.broadcasted_iota(jnp.int32, (n, n), 1)
     scale = 1.0 + 3.0 * act_v[...].astype(F32)
@@ -146,13 +187,40 @@
     weighted = resid_v[...] * scale
     weighted_v[...] = weighted
     solve_s[...] = dot(inv_v[...], weighted.astype(BF16)).astype(BF16)
-    for xx in (0, 1, 2, 3):
-        for kk in (0, 1):
-            ring_copy(
-                solve_s.at[:, lanes(xx)], solve_r.at[x_lo, :, lanes(period)], solve_sem.at[period * 2 + x_lo], xx, kk
-            )
-
-    load_start.wait()
+    landed(sens_half.at[x_lo], load_sem.at[0])
+    pl.semaphore_wait(barrier, 22)
+
+    half = sens_half.shape[1] // 2
+    for i, step in enumerate((1, X - 1)):
+        rows = pl.ds(i * half, half)
+        far_copy(
+            sens_half.at[x_lo, rows], sens_half.at[x_lo, rows], sens_sem.at[i], lax.rem(x + step, X), core
+        )
+
+    def sens_wait():
+        for i in range(2):
+            rows = pl.ds(i * half, half)
+            landed(sens_half.at[1 - x_lo, rows], sens_sem.at[i])
+
+    pend['sens'] = sens_wait
+
+    line = [(xx, kk) for xx in range(X) for kk in range(2)]
+    send_solve = ring_group('solve', [
+        (solve_s.at[:, lanes(xx)], solve_r.at[x_lo, :, lanes(period)], solve_sem.at[period * 2 + x_lo], xx, kk)
+        for xx, kk in line
+    ])
+    send_gain = ring_group('gain', [
+        (gain_s.at[kk], gain_r.at[period, x_lo], gain_sem.at[period * 2 + x_lo], xx, kk) for xx, kk in line
+    ])
+    send_schur = ring_group('schur', [
+        (schur_s.at[kk], schur_r.at[period, x_lo], schur_sem.at[period * 2 + x_lo], xx, kk) for xx, kk in line
+    ])
+    send_solve(3)
+
+    for t in range(T):
+        for j in range(2):
+            pend[f'solve{t}{j}'] = lambda t=t, j=j: landed(solve_r.at[j, :, lanes(t)], solve_sem.at[t * 2 + j])
+    take('load_start')
     start_b[...] = start_v[...].astype(BF16)
     own = x_lo == core
 
@@ -162,26 +230,28 @@
 
     far_copy(start_b.at[:, lanes(x_pair)], state_g.at[0, spot], first_sem.at[0], x_pair, core, own)
 
+    def first_wait():
+        @pl.when(jnp.logical_not(own))
+        def _():
+            landed(state_g.at[0, spot], first_sem.at[0])
+
+    pend['first'] = first_wait
+    for t in range(T):
+        pend[f'rhs{t}'] = lambda t=t: landed(rhs_r.at[t], rhs_sem.at[t])
     for xx in range(X):
         ring_copy(rhs.at[0, :, lanes(xx)], rhs_r.at[period], rhs_sem.at[period], xx, x_lo)
 
-    landed(gain_s, load_sem.at[6])
-    for xx in range(X):
-        for kk in range(2):
-            ring_copy(gain_s.at[kk], gain_r.at[period, x_lo], gain_sem.at[period * 2 + x_lo], xx, kk)
-
-    @pl.when(jnp.logical_not(own))
-    def _():
-        landed(state_g.at[0, spot], first_sem.at[0])
-
+    for t in range(T):
+        for j in range(2):
+            pend[f'gain{t}{j}'] = lambda t=t, j=j: landed(gain_r.at[t, j], gain_sem.at[t * 2 + j])
+    take('first')
+    pend['xg0'] = lambda: plane_wait(state_g.at[0], xg_sem.at[0])
     plane_copy(lambda ss: state_g.at[0, spot], state_g.at[0, spot], xg_sem.at[0])
 
-    landed(schur_s, load_sem.at[7])
-    for xx in range(X):
-        for kk in range(2):
-            ring_copy(schur_s.at[kk], schur_r.at[period, x_lo], schur_sem.at[period * 2 + x_lo], xx, kk)
-
-    load_ubus.wait()
+    for t in range(T):
+        for j in range(2):
+            pend[f'schur{t}{j}'] = lambda t=t, j=j: landed(schur_r.at[t, j], schur_sem.at[t * 2 + j])
+    take('load_ubus')
     for i in range(4):
         units = ubus_v[:, pl.ds(pl.multiple_of(i * 512 + core * 256, 256), 256)]
         for j in range(2):
@@ -191,101 +261,139 @@
                 ids == jnp.broadcast_to(units, (n, 256)), 1.0, 0.0
             ).astype(BF16)
 
-    for i in range(2):
-        rows = pl.ds(i * half, half)
-        landed(sens_half.at[1 - x_lo, rows], sens_sem.at[i])
+    take('sens')
+    take('gain_s')
+    take('schur_s')
+    send_solve(0, 1, 2)
+    send_gain(2)
     for j in range(2):
         sens_t[j] = sens_half[j].T
-    for t in range(T):
-        for j in range(2):
-            landed(solve_r.at[j, :, lanes(t)], solve_sem.at[t * 2 + j])
+    take('solve30')
+    take('solve31')
 
     def reduce_start(t, partial):
+        pend[f'rs{t}'] = lambda: plane_wait(rs_r.at[t], rs_sem.at[t])
         rs_s[t] = partial.astype(BF16).reshape(S, 64, cols)
         plane_copy(lambda ss: rs_s.at[t, ss], rs_r.at[t, spot], rs_sem.at[t])
         rs_r[t, spot] = rs_s[t, spot]
 
     last = (T - 1) * cols
     reduce_start(T - 1, dot(sens_t[0], solve_r[0, :, last:]) + dot(sens_t[1], solve_r[1, :, last:]))
+    send_gain(1)
+    for t in range(T - 1):
+        for j in range(2):
+            take(f'solve{t}{j}')
     part_v[...] = dot(sens_t[0], solve_r[0, :, :last]) + dot(sens_t[1], solve_r[1, :, :last])
+
+    def send_cg(t):
+        pend[f'cg{t}'] = lambda: plane_wait(cost_g.at[t], cg_sem.at[t])
+        plane_copy(lambda ss: cost_g.at[t, spot], cost_g.at[t, spot], cg_sem.at[t])
 
     for t in reversed(range(T)):
         if t < T - 1:
             for j in range(2):
-                landed(gain_r.at[t, j], gain_sem.at[t * 2 + j])
+                take(f'gain{t}{j}')
                 gain_t[t, :, j * 64 : (j + 1) * 64] = gain_r[t, j].T
-            landed(cost_p.at[t + 1, 1 - core], pair_sem.at[t + 1])
+            take(f'pair{t + 1}')
             reduce_start(
                 t, part_v[:, t * cols : (t + 1) * cols] + dot(gain_t[t], cost_p[t + 1].reshape(2 * 64, cols))
             )
-            plane_copy(lambda ss, t=t: cost_g.at[t + 1, spot], cost_g.at[t + 1, spot], cg_sem.at[t + 1])
-        landed(rhs_r.at[t], rhs_sem.at[t])
-        plane_wait(rs_r.at[t], rs_sem.at[t])
+        take(f'rhs{t}')
+        take(f'rs{t}')
         total = rhs_r[t] + jnp.sum(rs_r[t].astype(F32), axis=0)
         cost_v[t] = total
         rounded = total.astype(BF16)
         cost_g[t, spot] = rounded
         if t > 0:
             cost_p[t, core] = rounded
+            pend[f'pair{t}'] = lambda t=t: landed(cost_p.at[t, 1 - core], pair_sem.at[t])
             far_copy(cost_g.at[t, spot], cost_p.at[t, core], pair_sem.at[t], x, 1 - core)
         else:
-            plane_copy(lambda ss: cost_g.at[0, spot], cost_g.at[0, spot], cg_sem.at[0])
+            send_cg(0)
+            send_cg(1)
+        pend[f'cout{t}'] = lambda t=t: home_wait(t, lambda: [landed(cost_out.at[0, :, lanes(xx)], cout_sem.at[xx]) for xx in range(X)])
         ring_copy(cost_v.at[t], cost_out.at[0, :, lanes(x)], cout_sem.at[x], 2 * (t // 2) + core, t % 2)
+        if t == 3:
+            send_gain(0)
+        elif t == 2:
+            send_schur(0)
+        elif t == 1:
+            send_schur(1)
+        else:
+            send_schur(2)
 
     for t in range(T):
         for j in range(2):
             if t == T - 1:
-                landed(gain_r.at[t, j], gain_sem.at[t * 2 + j])
-            landed(schur_r.at[t, j], schur_sem.at[t * 2 + j])
+                take(f'gain{t}{j}')
+            take(f'schur{t}{j}')
         width = S * 64
-        plane_wait(state_g.at[t], xg_sem.at[t])
+        take(f'xg{t}')
         if t == T - 1:
             moved = dot(onehot[...], state_g[t].reshape(width, cols))
             inj_s[t] = moved.astype(BF16).reshape(2, n, cols)
             for j in range(2):
+                pend[f'inj{t}'] = lambda t=t: home_wait(t, inj_wait)
                 ring_copy(
                     inj_s.at[t, j], inj_r.at[core, :, lanes(x)], inj_sem.at[x * 2 + core], 2 * (t // 2) + j, t % 2
                 )
-        plane_wait(cost_g.at[t], cg_sem.at[t])
+        take(f'cg{t}')
         full = dot(gain_r[t].reshape(2 * 64, width), state_g[t].reshape(width, cols)) - dot(
             schur_r[t].reshape(2 * 64, width), cost_g[t].reshape(width, cols)
         )
         full_v[t] = full.reshape(2, 64, cols)
+        pend[f'full{t}'] = lambda t=t: landed(full_r.at[t], full_sem.at[t])
         far_copy(full_v.at[t, 1 - core], full_r.at[t], full_sem.at[t], x, 1 - core)
-        if t < T - 1:
-            moved = dot(onehot[...], state_g[t].reshape(width, cols))
-            inj_s[t] = moved.astype(BF16).reshape(2, n, cols)
-        landed(full_r.at[t], full_sem.at[t])
+        take(f'full{t}')
         total = full_v[t, core] + full_r[t]
         state_v[t] = total
         if t < T - 1:
             state_g[t + 1, spot] = total.astype(BF16)
+            pend[f'xg{t + 1}'] = lambda t=t: plane_wait(state_g.at[t + 1], xg_sem.at[t + 1])
             plane_copy(lambda ss, t=t: state_g.at[t + 1, spot], state_g.at[t + 1, spot], xg_sem.at[t + 1])
+            if t + 2 < T:
+                send_cg(t + 2)
+        pend[f'sout{t}'] = lambda t=t: home_wait(t, lambda: [landed(stor_out.at[0, :, lanes(xx)], sout_sem.at[xx]) for xx in range(X)])
         ring_copy(state_v.at[t], stor_out.at[0, :, lanes(x)], sout_sem.at[x], 2 * (t // 2) + core, t % 2)
+        if t == 0:
+            send_gain(3)
+            send_schur(3)
         if t < T - 1:
+            moved = dot(onehot[...], state_g[t].reshape(width, cols))
+            inj_s[t] = moved.astype(BF16).reshape(2, n, cols)
             for j in range(2):
+                pend[f'inj{t}'] = lambda t=t: home_wait(t, inj_wait)
                 ring_copy(
                     inj_s.at[t, j], inj_r.at[core, :, lanes(x)], inj_sem.at[x * 2 + core], 2 * (t // 2) + j, t % 2
                 )
 
-    for xx in range(X):
-        for kk in range(2):
-            landed(inj_r.at[kk, :, lanes(xx)], inj_sem.at[xx * 2 + kk])
+    for t in range(T):
+        take(f'inj{t}')
     network = weighted_v[...] - (inj_r[0].astype(F32) + inj_r[1].astype(F32))
     upd_v[...] = dot(inv_v[...], network.astype(BF16))
     store = pltpu.make_async_copy(upd_v, upd_out.at[0], load_sem.at[8])
     store.start()
-    for xx in range(X):
-        landed(cost_out.at[0, :, lanes(xx)], cout_sem.at[xx])
-        landed(stor_out.at[0, :, lanes(xx)], sout_sem.at[xx])
-    for on, copy in sent:
+    for t in range(T):
+        take(f'cout{t}')
+        take(f'sout{t}')
+    store.wait()
+
+    for key in list(pend):
+        take(key)
+    for on, copy, *more in sent:
+        if more:
+            if not more[0]:
+                continue
+            had = period == more[0][0]
+            for p in more[0][1:]:
+                had = had | (period == p)
+            on = on & had
         if on is None:
             copy.wait_send()
         else:
             pl.when(on)(copy.wait_send)
     for send in plane_sent:
         plane_wait(rs_s.at[0], send)
-    store.wait()
 
 
 def body(gain, schur, inverse_blocks, sensitivity, residual_bus, unit_rhs, start_state, active_set, unit_bus):
@@ -353,7 +461,7 @@
         out_specs=(anywhere,) * 3,
         scratch_shapes=scratch,
         compiler_params=pltpu.CompilerParams(
-            collective_id=0, has_side_effects=True, vmem_limit_bytes=48 * 1024 * 1024
+            collective_id=0, has_side_effects=True, vmem_limit_bytes=60 * 1024 * 1024
         ),
     )(
         gain, schur, inverse_blocks, sensitivity, residual_bus, unit_rhs, start_state, active_set,

time: 111 us -> 95.1 us (0.86)
  Pallas kernels: 99.8 us -> 89.1 us
  local copies, waits for them, and re-layouts: 10.6 us -> 5.1 us
    pallas_call x1, Pallas kernels: 99.8 us -> 89.1 us  [body(): pl.pallas_call(kernel, out_shape=(jax.ShapeDtypeStruct((1, 64, 512), F32)...]
    unnamed x21 -> x3, local copies, waits for them, and re-layouts: 10.6 us -> 5.1 us
where the time goes in v2:
time: 95.1 us; the launch traced here: 94.8 us
  Pallas kernels  89.1 us (94%)
  local copies, waits for them, and re-layouts  5.1 us (5%)
    pallas_call x1, Pallas kernels, body(): pl.pallas_call(kernel, out_shape=(jax.ShapeDtypeStruct((1, 64, 512), F32)...  89.1 us
    unnamed x3, local copies, waits for them, and re-layouts  5.1 us

profile of v2, /device:TPU:7, one launch (start us, length us, event | category | flops | bytes accessed | tf_op | source)
XLA Modules:
  0.0 94.8 jit_solution(4520833472377849594)
XLA Ops:
  0.6 89.1 %shard_map.112 = (f32[1,64,512]{2,1,0:T(8,128)}, f32[1,64,512]{2,1,0:T(8,128)}, f32[1,320,512]{2,1,0:T(8,128)}) custom-call(bf16[1,64,2048]{2,1,0:T(8,128)(2,1)} %gain.1, bf16[1,64,2048]{2,1,0:T(8,128)(2,1)} %schur.1, bf16[1,320,320]{2,1,0:T(8,128)(2,1)} %inverse.1, bf16[320,2048]{1,0:T(8,128)(2,1)} %sens.1, f32[1,320,512]{2,1,0:T(8,128)} %resid.1, ...), custom_call_target="tpu_custom_call" | custom-call | tf_op jit(solution)/shard_map/pallas_call | solution.py:453
  89.7 1.6 %copy.15 = f32[1,64,512]{2,1,0:T(8,128)} copy(f32[1,64,512]{2,1,0:T(8,128)} %get-tuple-element.6) | data formatting | bytes 262144
  91.3 1.6 %copy.16 = f32[1,64,512]{2,1,0:T(8,128)} copy(f32[1,64,512]{2,1,0:T(8,128)} %get-tuple-element.7) | data formatting | bytes 262144
  92.9 2.0 %copy.17 = f32[1,320,512]{2,1,0:T(8,128)} copy(f32[1,320,512]{2,1,0:T(8,128)} %get-tuple-element.8) | data formatting | bytes 1310720

commit v3 on v2

--- a/solution.py
+++ b/solution.py
@@ -10,6 +10,9 @@
 X = 4
 S = 16
 F32 = jnp.float32
+OTHERS = sorted(
+    ((dz, dy) for dz in range(4) for dy in range(4) if dz or dy), key=lambda d: -min(d[0], 4 - d[0]) - min(d[1], 4 - d[1])
+)
 BF16 = jnp.bfloat16
 
 
@@ -19,11 +22,11 @@
 
 def kernel(
     gain, schur, inverse, sens, resid, rhs, start, active, unit_bus,
-    stor_out, cost_out, upd_out,
+    stor_out, cost_out, network_out,
     sens_half, sens_t, resid_v, inv_v, act_v, ubus_v, start_v, start_b, weighted_v, solve_s, solve_r,
     gain_s, schur_s, gain_r, schur_r, gain_t, rhs_r, part_v, rs_s, rs_r, cost_v, cost_g, cost_p,
-    state_v, state_g, full_v, full_r, onehot, inj_s, inj_r, upd_v,
-    load_sem, sens_sem, solve_sem, gain_sem, schur_sem, rhs_sem, first_sem, rs_sem, cg_sem, xg_sem, pair_sem, full_sem,
+    state_v, state_g, full_v, full_r, onehot, inj_s, inj_r, network_v,
+    load_sem, sens_sem, solve_sem, swap_sem, gain_sem, schur_sem, rhs_sem, first_sem, rs_sem, cg_sem, xg_sem, pair_sem, full_sem,
     inj_sem, cout_sem, sout_sem, send_ring, send_plane,
 ):
     period = lax.axis_index("period")
@@ -40,6 +43,9 @@
 
     def plane_id(ss):
         return (period, lax.div(ss, 4) * 8 + x_lo * 4 + lax.rem(ss, 4))
+
+    def plane_spot(dz, dy):
+        return lax.rem(z + dz, 4) * 4 + lax.rem(y + dy, 4)
 
     def lanes(xx):
         return pl.ds(pl.multiple_of(xx * cols, cols), cols)
@@ -109,14 +115,11 @@
     def plane_copy(src_at, dst, recv):
         send = send_plane.at[len(plane_sent)]
 
-        def one(i, carry):
-            ss = lax.rem(spot + i, S)
+        for dz, dy in OTHERS:
+            ss = plane_spot(dz, dy)
             pltpu.make_async_remote_copy(
                 src_ref=src_at(ss), dst_ref=dst, send_sem=send, recv_sem=recv, device_id=plane_id(ss), device_id_type=MESH
             ).start()
-            return carry
-
-        lax.fori_loop(1, S, one, 0)
         plane_sent.append(send)
 
     def plane_wait(buf, sem):
@@ -141,17 +144,17 @@
                 landed(inj_r.at[kk, :, lanes(xx)], inj_sem.at[xx * 2 + kk])
 
     barrier = pltpu.get_barrier_semaphore()
-    for i in range(1, 8):
-        there = lax.rem(x * 2 + core + i, 8)
-        pl.semaphore_signal(
-            barrier, inc=1, device_id=ring_id(lax.div(there, 2), lax.rem(there, 2)), device_id_type=MESH
-        )
-
-    def greet(i, carry):
-        pl.semaphore_signal(barrier, inc=1, device_id=plane_id(lax.rem(spot + i, S)), device_id_type=MESH)
-        return carry
-
-    lax.fori_loop(1, S, greet, 0)
+    def greet(device):
+        pl.semaphore_signal(barrier, inc=1, device_id=device, device_id_type=MESH)
+
+    for i in range(10):
+        greet(plane_id(plane_spot(*OTHERS[i])))
+    for dx in (2, 1, 3):
+        for kk in range(2):
+            greet(ring_id(lax.rem(x + dx, X), kk))
+    for i in range(10, S - 1):
+        greet(plane_id(plane_spot(*OTHERS[i])))
+    greet(ring_id(x, 1 - core))
 
     for i in range(4):
         strip = pl.ds(pl.multiple_of(i * 512 + core * 256, 256), 256)
@@ -206,8 +209,17 @@
 
     line = [(xx, kk) for xx in range(X) for kk in range(2)]
     send_solve = ring_group('solve', [
-        (solve_s.at[:, lanes(xx)], solve_r.at[x_lo, :, lanes(period)], solve_sem.at[period * 2 + x_lo], xx, kk)
+        (
+            solve_s.at[kk * half : (kk + 1) * half, lanes(xx)],
+            solve_r.at[x_lo, kk * half : (kk + 1) * half, lanes(period)],
+            solve_sem.at[period * 2 + x_lo],
+            xx,
+            kk,
+        )
         for xx, kk in line
+    ])
+    send_rhs = ring_group('rhs', [
+        (rhs.at[0, :, lanes(xx)], rhs_r.at[period], rhs_sem.at[period], xx, x_lo) for xx in range(X)
     ])
     send_gain = ring_group('gain', [
         (gain_s.at[kk], gain_r.at[period, x_lo], gain_sem.at[period * 2 + x_lo], xx, kk) for xx, kk in line
@@ -215,11 +227,24 @@
     send_schur = ring_group('schur', [
         (schur_s.at[kk], schur_r.at[period, x_lo], schur_sem.at[period * 2 + x_lo], xx, kk) for xx, kk in line
     ])
+    def half_solve(t, j, kk):
+        return solve_r.at[j, pl.ds(pl.multiple_of(kk * half, 32), half), lanes(t)]
+
+    def swap_solve(*periods):
+        for t in periods:
+            for j in range(2):
+                take(f'solve{t}{j}')
+                pend[f'swap{t}{j}'] = lambda t=t, j=j: landed(half_solve(t, j, 1 - core), swap_sem.at[t * 2 + j])
+                far_copy(half_solve(t, j, core), half_solve(t, j, core), swap_sem.at[t * 2 + j], x, 1 - core)
+        for t in periods:
+            for j in range(2):
+                take(f'swap{t}{j}')
+
     send_solve(3)
 
     for t in range(T):
         for j in range(2):
-            pend[f'solve{t}{j}'] = lambda t=t, j=j: landed(solve_r.at[j, :, lanes(t)], solve_sem.at[t * 2 + j])
+            pend[f'solve{t}{j}'] = lambda t=t, j=j: landed(half_solve(t, j, core), solve_sem.at[t * 2 + j])
     take('load_start')
     start_b[...] = start_v[...].astype(BF16)
     own = x_lo == core
@@ -238,8 +263,7 @@
     pend['first'] = first_wait
     for t in range(T):
         pend[f'rhs{t}'] = lambda t=t: landed(rhs_r.at[t], rhs_sem.at[t])
-    for xx in range(X):
-        ring_copy(rhs.at[0, :, lanes(xx)], rhs_r.at[period], rhs_sem.at[period], xx, x_lo)
+    send_rhs(3)
 
     for t in range(T):
         for j in range(2):
@@ -261,15 +285,14 @@
                 ids == jnp.broadcast_to(units, (n, 256)), 1.0, 0.0
             ).astype(BF16)
 
-    take('sens')
+    sens_t[x_lo] = sens_half[x_lo].T
     take('gain_s')
     take('schur_s')
     send_solve(0, 1, 2)
-    send_gain(2)
-    for j in range(2):
-        sens_t[j] = sens_half[j].T
-    take('solve30')
-    take('solve31')
+    send_gain(1, 2)
+    take('sens')
+    sens_t[1 - x_lo] = sens_half[1 - x_lo].T
+    swap_solve(3)
 
     def reduce_start(t, partial):
         pend[f'rs{t}'] = lambda: plane_wait(rs_r.at[t], rs_sem.at[t])
@@ -279,10 +302,8 @@
 
     last = (T - 1) * cols
     reduce_start(T - 1, dot(sens_t[0], solve_r[0, :, last:]) + dot(sens_t[1], solve_r[1, :, last:]))
-    send_gain(1)
-    for t in range(T - 1):
-        for j in range(2):
-            take(f'solve{t}{j}')
+    send_rhs(0, 1, 2)
+    swap_solve(0, 1, 2)
     part_v[...] = dot(sens_t[0], solve_r[0, :, :last]) + dot(sens_t[1], solve_r[1, :, :last])
 
     def send_cg(t):
@@ -291,13 +312,20 @@
 
     for t in reversed(range(T)):
         if t < T - 1:
-            for j in range(2):
-                take(f'gain{t}{j}')
-                gain_t[t, :, j * 64 : (j + 1) * 64] = gain_r[t, j].T
             take(f'pair{t + 1}')
             reduce_start(
                 t, part_v[:, t * cols : (t + 1) * cols] + dot(gain_t[t], cost_p[t + 1].reshape(2 * 64, cols))
             )
+            if t == 2:
+                send_gain(0, 3)
+            elif t == 1:
+                send_schur(0, 2)
+            else:
+                send_schur(1, 3)
+        if t > 0:
+            for j in range(2):
+                take(f'gain{t - 1}{j}')
+                gain_t[t - 1, :, j * 64 : (j + 1) * 64] = gain_r[t - 1, j].T
         take(f'rhs{t}')
         take(f'rs{t}')
         total = rhs_r[t] + jnp.sum(rs_r[t].astype(F32), axis=0)
@@ -313,14 +341,6 @@
             send_cg(1)
         pend[f'cout{t}'] = lambda t=t: home_wait(t, lambda: [landed(cost_out.at[0, :, lanes(xx)], cout_sem.at[xx]) for xx in range(X)])
         ring_copy(cost_v.at[t], cost_out.at[0, :, lanes(x)], cout_sem.at[x], 2 * (t // 2) + core, t % 2)
-        if t == 3:
-            send_gain(0)
-        elif t == 2:
-            send_schur(0)
-        elif t == 1:
-            send_schur(1)
-        else:
-            send_schur(2)
 
     for t in range(T):
         for j in range(2):
@@ -328,7 +348,14 @@
                 take(f'gain{t}{j}')
             take(f'schur{t}{j}')
         width = S * 64
-        take(f'xg{t}')
+        if t == 0:
+            take('xg0')
+            moving = dot(gain_r[t].reshape(2 * 64, width), state_g[t].reshape(width, cols))
+            take('cg0')
+        else:
+            take(f'cg{t}')
+            pushed = dot(schur_r[t].reshape(2 * 64, width), cost_g[t].reshape(width, cols))
+            take(f'xg{t}')
         if t == T - 1:
             moved = dot(onehot[...], state_g[t].reshape(width, cols))
             inj_s[t] = moved.astype(BF16).reshape(2, n, cols)
@@ -337,10 +364,11 @@
                 ring_copy(
                     inj_s.at[t, j], inj_r.at[core, :, lanes(x)], inj_sem.at[x * 2 + core], 2 * (t // 2) + j, t % 2
                 )
-        take(f'cg{t}')
-        full = dot(gain_r[t].reshape(2 * 64, width), state_g[t].reshape(width, cols)) - dot(
-            schur_r[t].reshape(2 * 64, width), cost_g[t].reshape(width, cols)
-        )
+        if t == 0:
+            pushed = dot(schur_r[t].reshape(2 * 64, width), cost_g[t].reshape(width, cols))
+        else:
+            moving = dot(gain_r[t].reshape(2 * 64, width), state_g[t].reshape(width, cols))
+        full = moving - pushed
         full_v[t] = full.reshape(2, 64, cols)
         pend[f'full{t}'] = lambda t=t: landed(full_r.at[t], full_sem.at[t])
         far_copy(full_v.at[t, 1 - core], full_r.at[t], full_sem.at[t], x, 1 - core)
@@ -355,9 +383,6 @@
                 send_cg(t + 2)
         pend[f'sout{t}'] = lambda t=t: home_wait(t, lambda: [landed(stor_out.at[0, :, lanes(xx)], sout_sem.at[xx]) for xx in range(X)])
         ring_copy(state_v.at[t], stor_out.at[0, :, lanes(x)], sout_sem.at[x], 2 * (t // 2) + core, t % 2)
-        if t == 0:
-            send_gain(3)
-            send_schur(3)
         if t < T - 1:
             moved = dot(onehot[...], state_g[t].reshape(width, cols))
             inj_s[t] = moved.astype(BF16).reshape(2, n, cols)
@@ -370,8 +395,8 @@
     for t in range(T):
         take(f'inj{t}')
     network = weighted_v[...] - (inj_r[0].astype(F32) + inj_r[1].astype(F32))
-    upd_v[...] = dot(inv_v[...], network.astype(BF16))
-    store = pltpu.make_async_copy(upd_v, upd_out.at[0], load_sem.at[8])
+    network_v[...] = network.astype(BF16)
+    store = pltpu.make_async_copy(network_v, network_out, load_sem.at[8])
     store.start()
     for t in range(T):
         take(f'cout{t}')
@@ -394,6 +419,24 @@
             pl.when(on)(copy.wait_send)
     for send in plane_sent:
         plane_wait(rs_s.at[0], send)
+
+
+def finish(stor, cost, network, inverse, stor_out, cost_out, upd_out, stor_v, cost_v, network_v, inv_v, upd_v, sem):
+    pairs = ((network, network_v), (inverse, inv_v), (stor, stor_v), (cost, cost_v))
+    loads = [pltpu.make_async_copy(src, dst, sem.at[i]) for i, (src, dst) in enumerate(pairs)]
+    for load in loads:
+        load.start()
+    loads[0].wait()
+    loads[1].wait()
+    upd_v[0] = dot(inv_v[0], network_v[...])
+    stores = [pltpu.make_async_copy(upd_v, upd_out, sem.at[4])]
+    stores[0].start()
+    for i, (src, dst) in enumerate(((stor_v, stor_out), (cost_v, cost_out))):
+        loads[2 + i].wait()
+        stores.append(pltpu.make_async_copy(src, dst, sem.at[5 + i]))
+        stores[-1].start()
+    for copy in stores:
+        copy.wait()
 
 
 def body(gain, schur, inverse_blocks, sensitivity, residual_bus, unit_rhs, start_state, active_set, unit_bus):
@@ -431,12 +474,13 @@
         pltpu.VMEM((2 * n, 1024), BF16),
         pltpu.VMEM((T, 2, n, 128), BF16),
         pltpu.VMEM((2, n, 512), BF16),
-        pltpu.VMEM((n, 512), F32),
+        pltpu.VMEM((n, 512), BF16),
         dma((9,)),
         dma((2,)),
         dma((8,)),
         dma((8,)),
         dma((8,)),
+        dma((8,)),
         dma((4,)),
         dma((1,)),
         dma((4,)),
@@ -447,15 +491,15 @@
         dma((8,)),
         dma((4,)),
         dma((4,)),
-        dma((64,)),
+        dma((80,)),
         dma((12,)),
     ]
-    return pl.pallas_call(
+    moved = pl.pallas_call(
         kernel,
         out_shape=(
             jax.ShapeDtypeStruct((1, 64, 512), F32),
             jax.ShapeDtypeStruct((1, 64, 512), F32),
-            jax.ShapeDtypeStruct((1, n, 512), F32),
+            jax.ShapeDtypeStruct((n, 512), BF16),
         ),
         in_specs=[anywhere] * 9,
         out_specs=(anywhere,) * 3,
@@ -467,6 +511,25 @@
         gain, schur, inverse_blocks, sensitivity, residual_bus, unit_rhs, start_state, active_set,
         unit_bus.reshape(1, -1),
     )
+    return pl.pallas_call(
+        finish,
+        out_shape=(
+            jax.ShapeDtypeStruct((1, 64, 512), F32),
+            jax.ShapeDtypeStruct((1, 64, 512), F32),
+            jax.ShapeDtypeStruct((1, n, 512), F32),
+        ),
+        in_specs=[anywhere] * 4,
+        out_specs=(anywhere,) * 3,
+        scratch_shapes=[
+            pltpu.VMEM((1, 64, 512), F32),
+            pltpu.VMEM((1, 64, 512), F32),
+            pltpu.VMEM((n, 512), BF16),
+            pltpu.VMEM((1, n, n), BF16),
+            pltpu.VMEM((1, n, 512), F32),
+            dma((7,)),
+        ],
+        compiler_params=pltpu.CompilerParams(vmem_limit_bytes=60 * 1024 * 1024),
+    )(*moved, inverse_blocks)
 
 
 def solution(mesh):

time: 95.1 us -> 86.5 us (0.910)
  local copies, waits for them, and re-layouts: 5.1 us -> 0 us
  Pallas kernels: 89.1 us -> 85.7 us
    pallas_call x1, Pallas kernels: 89.1 us -> 83.3 us  [body(): pl.pallas_call(kernel, out_shape=(jax.ShapeDtypeStruct((1, 64, 512), F32)...]
    unnamed x3 -> x0, local copies, waits for them, and re-layouts: 5.1 us -> none
    pallas_call x0 -> x1, Pallas kernels: none -> 2.35 us  [body(): pl.pallas_call(finish, out_shape=(jax.ShapeDtypeStruct((1, 64, 512), F32)...]
where the time goes in v3:
time: 86.5 us; the launch traced here: 86.3 us
  Pallas kernels  85.7 us (99%)
    pallas_call x1, Pallas kernels, body(): pl.pallas_call(kernel, out_shape=(jax.ShapeDtypeStruct((1, 64, 512), F32)...  83.3 us
    pallas_call x1, Pallas kernels, body(): pl.pallas_call(finish, out_shape=(jax.ShapeDtypeStruct((1, 64, 512), F32)...  2.35 us

profile of v3, /device:TPU:7, one launch (start us, length us, event | category | flops | bytes accessed | tf_op | source)
XLA Modules:
  0.0 86.3 jit_solution(11661716070963576522)
XLA Ops:
  0.6 83.3 %shard_map.112 = (f32[1,64,512]{2,1,0:T(8,128)}, f32[1,64,512]{2,1,0:T(8,128)}, bf16[320,512]{1,0:T(8,128)(2,1)}) custom-call(bf16[1,64,2048]{2,1,0:T(8,128)(2,1)} %gain.1, bf16[1,64,2048]{2,1,0:T(8,128)(2,1)} %schur.1, bf16[1,320,320]{2,1,0:T(8,128)(2,1)} %inverse.3, bf16[320,2048]{1,0:T(8,128)(2,1)} %sens.1, f32[1,320,512]{2,1,0:T(8,128)} %resid.1, ...), custom_call_target="tpu_custom_call" | custom-call | tf_op jit(solution)/shard_map/pallas_call | solution.py:497
  84.0 2.3 %shard_map.113 = (f32[1,64,512]{2,1,0:T(8,128)}, f32[1,64,512]{2,1,0:T(8,128)}, f32[1,320,512]{2,1,0:T(8,128)}) custom-call(f32[1,64,512]{2,1,0:T(8,128)} %get-tuple-element.6.stor, f32[1,64,512]{2,1,0:T(8,128)} %get-tuple-element.7.cost, bf16[320,512]{1,0:T(8,128)(2,1)} %get-tuple-element.8.network, bf16[1,320,320]{2,1,0:T(8,128)(2,1)} %inverse.3), custom_call_target="tpu_custom_call" | custom-call | tf_op jit(solution)/shard_map/pallas_call | solution.py:514

commit v4 on v3

--- a/solution.py
+++ b/solution.py
@@ -25,9 +25,9 @@
     stor_out, cost_out, network_out,
     sens_half, sens_t, resid_v, inv_v, act_v, ubus_v, start_v, start_b, weighted_v, solve_s, solve_r,
     gain_s, schur_s, gain_r, schur_r, gain_t, rhs_r, part_v, rs_s, rs_r, cost_v, cost_g, cost_p,
-    state_v, state_g, full_v, full_r, onehot, inj_s, inj_r, network_v,
+    state_v, state_g, full_v, full_r, onehot, inj_s, inj_p, inj_r, network_v,
     load_sem, sens_sem, solve_sem, swap_sem, gain_sem, schur_sem, rhs_sem, first_sem, rs_sem, cg_sem, xg_sem, pair_sem, full_sem,
-    inj_sem, cout_sem, sout_sem, send_ring, send_plane,
+    inj_sem, injp_sem, cout_sem, sout_sem, send_ring, send_plane,
 ):
     period = lax.axis_index("period")
     bus = lax.axis_index("bus")
@@ -140,8 +140,7 @@
 
     def inj_wait():
         for xx in range(X):
-            for kk in range(2):
-                landed(inj_r.at[kk, :, lanes(xx)], inj_sem.at[xx * 2 + kk])
+            landed(inj_r.at[:, lanes(xx)], inj_sem.at[xx])
 
     barrier = pltpu.get_barrier_semaphore()
     def greet(device):
@@ -296,12 +295,24 @@
 
     def reduce_start(t, partial):
         pend[f'rs{t}'] = lambda: plane_wait(rs_r.at[t], rs_sem.at[t])
-        rs_s[t] = partial.astype(BF16).reshape(S, 64, cols)
-        plane_copy(lambda ss: rs_s.at[t, ss], rs_r.at[t, spot], rs_sem.at[t])
+        send = send_plane.at[len(plane_sent)]
+        plane_sent.append(send)
+        for dz in (2, 1, 3, 0):
+            zz = lax.rem(z + dz, 4)
+            block = partial(pl.ds(pl.multiple_of(zz * 256, 256), 256))
+            rs_s[t, pl.ds(zz * 4, 4)] = block.astype(BF16).reshape(4, 64, cols)
+            for dy in (2, 1, 3) if dz == 0 else (2, 1, 3, 0):
+                ss = plane_spot(dz, dy)
+                pltpu.make_async_remote_copy(
+                    src_ref=rs_s.at[t, ss], dst_ref=rs_r.at[t, spot], send_sem=send, recv_sem=rs_sem.at[t],
+                    device_id=plane_id(ss), device_id_type=MESH,
+                ).start()
         rs_r[t, spot] = rs_s[t, spot]
 
     last = (T - 1) * cols
-    reduce_start(T - 1, dot(sens_t[0], solve_r[0, :, last:]) + dot(sens_t[1], solve_r[1, :, last:]))
+    reduce_start(
+        T - 1, lambda rows: dot(sens_t[0, rows], solve_r[0, :, last:]) + dot(sens_t[1, rows], solve_r[1, :, last:])
+    )
     send_rhs(0, 1, 2)
     swap_solve(0, 1, 2)
     part_v[...] = dot(sens_t[0], solve_r[0, :, :last]) + dot(sens_t[1], solve_r[1, :, :last])
@@ -314,7 +325,9 @@
         if t < T - 1:
             take(f'pair{t + 1}')
             reduce_start(
-                t, part_v[:, t * cols : (t + 1) * cols] + dot(gain_t[t], cost_p[t + 1].reshape(2 * 64, cols))
+                t,
+                lambda rows, t=t: part_v[rows, t * cols : (t + 1) * cols]
+                + dot(gain_t[t, rows], cost_p[t + 1].reshape(2 * 64, cols)),
             )
             if t == 2:
                 send_gain(0, 3)
@@ -342,6 +355,17 @@
         pend[f'cout{t}'] = lambda t=t: home_wait(t, lambda: [landed(cost_out.at[0, :, lanes(xx)], cout_sem.at[xx]) for xx in range(X)])
         ring_copy(cost_v.at[t], cost_out.at[0, :, lanes(x)], cout_sem.at[x], 2 * (t // 2) + core, t % 2)
 
+    def inj_add(t):
+        inj_s[t, 1 - core] = dot(
+            onehot[pl.ds(pl.multiple_of((1 - core) * n, 64), n), :], state_g[t].reshape(S * 64, cols)
+        ).astype(BF16)
+        far_copy(inj_s.at[t, 1 - core], inj_p.at[t], injp_sem.at[t], x, 1 - core)
+        mine = dot(onehot[pl.ds(pl.multiple_of(core * n, 64), n), :], state_g[t].reshape(S * 64, cols))
+        landed(inj_p.at[t], injp_sem.at[t])
+        inj_s[t, core] = (mine + inj_p[t].astype(F32)).astype(BF16)
+        pend[f'inj{t}'] = lambda t=t: home_wait(t, inj_wait)
+        ring_copy(inj_s.at[t, core], inj_r.at[:, lanes(x)], inj_sem.at[x], 2 * (t // 2) + core, t % 2)
+
     for t in range(T):
         for j in range(2):
             if t == T - 1:
@@ -357,13 +381,7 @@
             pushed = dot(schur_r[t].reshape(2 * 64, width), cost_g[t].reshape(width, cols))
             take(f'xg{t}')
         if t == T - 1:
-            moved = dot(onehot[...], state_g[t].reshape(width, cols))
-            inj_s[t] = moved.astype(BF16).reshape(2, n, cols)
-            for j in range(2):
-                pend[f'inj{t}'] = lambda t=t: home_wait(t, inj_wait)
-                ring_copy(
-                    inj_s.at[t, j], inj_r.at[core, :, lanes(x)], inj_sem.at[x * 2 + core], 2 * (t // 2) + j, t % 2
-                )
+            inj_add(t)
         if t == 0:
             pushed = dot(schur_r[t].reshape(2 * 64, width), cost_g[t].reshape(width, cols))
         else:
@@ -384,17 +402,11 @@
         pend[f'sout{t}'] = lambda t=t: home_wait(t, lambda: [landed(stor_out.at[0, :, lanes(xx)], sout_sem.at[xx]) for xx in range(X)])
         ring_copy(state_v.at[t], stor_out.at[0, :, lanes(x)], sout_sem.at[x], 2 * (t // 2) + core, t % 2)
         if t < T - 1:
-            moved = dot(onehot[...], state_g[t].reshape(width, cols))
-            inj_s[t] = moved.astype(BF16).reshape(2, n, cols)
-            for j in range(2):
-                pend[f'inj{t}'] = lambda t=t: home_wait(t, inj_wait)
-                ring_copy(
-                    inj_s.at[t, j], inj_r.at[core, :, lanes(x)], inj_sem.at[x * 2 + core], 2 * (t // 2) + j, t % 2
-                )
+            inj_add(t)
 
     for t in range(T):
         take(f'inj{t}')
-    network = weighted_v[...] - (inj_r[0].astype(F32) + inj_r[1].astype(F32))
+    network = weighted_v[...] - inj_r[...].astype(F32)
     network_v[...] = network.astype(BF16)
     store = pltpu.make_async_copy(network_v, network_out, load_sem.at[8])
     store.start()
@@ -473,7 +485,8 @@
         pltpu.VMEM((T, 64, 128), F32),
         pltpu.VMEM((2 * n, 1024), BF16),
         pltpu.VMEM((T, 2, n, 128), BF16),
-        pltpu.VMEM((2, n, 512), BF16),
+        pltpu.VMEM((T, n, 128), BF16),
+        pltpu.VMEM((n, 512), BF16),
         pltpu.VMEM((n, 512), BF16),
         dma((9,)),
         dma((2,)),
@@ -488,7 +501,8 @@
         dma((4,)),
         dma((4,)),
         dma((4,)),
-        dma((8,)),
+        dma((4,)),
+        dma((4,)),
         dma((4,)),
         dma((4,)),
         dma((80,)),

time: 86.5 us -> 85.2 us (0.985)
  Pallas kernels: 85.7 us -> 84.4 us
    pallas_call x1, Pallas kernels: 83.3 us -> 82.1 us  [body(): pl.pallas_call(kernel, out_shape=(jax.ShapeDtypeStruct((1, 64, 512), F32)...]
where the time goes in v4:
time: 85.2 us; the launch traced here: 85.1 us
  Pallas kernels  84.4 us (99%)
    pallas_call x1, Pallas kernels, body(): pl.pallas_call(kernel, out_shape=(jax.ShapeDtypeStruct((1, 64, 512), F32)...  82.1 us
    pallas_call x1, Pallas kernels, body(): pl.pallas_call(finish, out_shape=(jax.ShapeDtypeStruct((1, 64, 512), F32)...  2.35 us

profile of v4, /device:TPU:7, one launch (start us, length us, event | category | flops | bytes accessed | tf_op | source)
XLA Modules:
  0.0 85.1 jit_solution(13566039282533791203)
XLA Ops:
  0.6 82.1 %shard_map.112 = (f32[1,64,512]{2,1,0:T(8,128)}, f32[1,64,512]{2,1,0:T(8,128)}, bf16[320,512]{1,0:T(8,128)(2,1)}) custom-call(bf16[1,64,2048]{2,1,0:T(8,128)(2,1)} %gain.1, bf16[1,64,2048]{2,1,0:T(8,128)(2,1)} %schur.1, bf16[1,320,320]{2,1,0:T(8,128)(2,1)} %inverse.3, bf16[320,2048]{1,0:T(8,128)(2,1)} %sens.1, f32[1,320,512]{2,1,0:T(8,128)} %resid.1, ...), custom_call_target="tpu_custom_call" | custom-call | tf_op jit(solution)/shard_map/pallas_call | solution.py:511
  82.7 2.3 %shard_map.113 = (f32[1,64,512]{2,1,0:T(8,128)}, f32[1,64,512]{2,1,0:T(8,128)}, f32[1,320,512]{2,1,0:T(8,128)}) custom-call(f32[1,64,512]{2,1,0:T(8,128)} %get-tuple-element.6.stor, f32[1,64,512]{2,1,0:T(8,128)} %get-tuple-element.7.cost, bf16[320,512]{1,0:T(8,128)(2,1)} %get-tuple-element.8.network, bf16[1,320,320]{2,1,0:T(8,128)(2,1)} %inverse.3), custom_call_target="tpu_custom_call" | custom-call | tf_op jit(solution)/shard_map/pallas_call | solution.py:528

commit v5 on v4

--- a/solution.py
+++ b/solution.py
@@ -193,16 +193,18 @@
     pl.semaphore_wait(barrier, 22)
 
     half = sens_half.shape[1] // 2
-    for i, step in enumerate((1, X - 1)):
-        rows = pl.ds(i * half, half)
-        far_copy(
-            sens_half.at[x_lo, rows], sens_half.at[x_lo, rows], sens_sem.at[i], lax.rem(x + step, X), core
-        )
+    cut_row = 176
+    pieces = (pl.ds(0, cut_row), pl.ds(cut_row, 2 * half - cut_row))
+    for hi, rows in enumerate(pieces):
+        for step in (1, X - 1):
+            far_copy(
+                sens_half.at[x_lo, rows], sens_half.at[x_lo, rows], sens_sem.at[hi], lax.rem(x + step, X), core,
+                x_hi == hi,
+            )
 
     def sens_wait():
-        for i in range(2):
-            rows = pl.ds(i * half, half)
-            landed(sens_half.at[1 - x_lo, rows], sens_sem.at[i])
+        for hi, rows in enumerate(pieces):
+            landed(sens_half.at[1 - x_lo, rows], sens_sem.at[hi])
 
     pend['sens'] = sens_wait
 
@@ -288,7 +290,7 @@
     take('gain_s')
     take('schur_s')
     send_solve(0, 1, 2)
-    send_gain(1, 2)
+    send_gain(2)
     take('sens')
     sens_t[1 - x_lo] = sens_half[1 - x_lo].T
     swap_solve(3)
@@ -314,6 +316,7 @@
         T - 1, lambda rows: dot(sens_t[0, rows], solve_r[0, :, last:]) + dot(sens_t[1, rows], solve_r[1, :, last:])
     )
     send_rhs(0, 1, 2)
+    send_gain(1)
     swap_solve(0, 1, 2)
     part_v[...] = dot(sens_t[0], solve_r[0, :, :last]) + dot(sens_t[1], solve_r[1, :, :last])
 

time: 85.2 us -> 84.6 us (level)
  Pallas kernels: 84.4 us -> 83.5 us
    pallas_call x1, Pallas kernels: 82.1 us -> 81.2 us  [body(): pl.pallas_call(kernel, out_shape=(jax.ShapeDtypeStruct((1, 64, 512), F32)...]
where the time goes in v5:
time: 84.6 us; the launch traced here: 84.1 us
  Pallas kernels  83.5 us (99%)
    pallas_call x1, Pallas kernels, body(): pl.pallas_call(kernel, out_shape=(jax.ShapeDtypeStruct((1, 64, 512), F32)...  81.2 us
    pallas_call x1, Pallas kernels, body(): pl.pallas_call(finish, out_shape=(jax.ShapeDtypeStruct((1, 64, 512), F32)...  2.35 us

profile of v5, /device:TPU:7, one launch (start us, length us, event | category | flops | bytes accessed | tf_op | source)
XLA Modules:
  0.0 84.1 jit_solution(4241152324403015695)
XLA Ops:
  0.6 81.2 %shard_map.112 = (f32[1,64,512]{2,1,0:T(8,128)}, f32[1,64,512]{2,1,0:T(8,128)}, bf16[320,512]{1,0:T(8,128)(2,1)}) custom-call(bf16[1,64,2048]{2,1,0:T(8,128)(2,1)} %gain.1, bf16[1,64,2048]{2,1,0:T(8,128)(2,1)} %schur.1, bf16[1,320,320]{2,1,0:T(8,128)(2,1)} %inverse.3, bf16[320,2048]{1,0:T(8,128)(2,1)} %sens.1, f32[1,320,512]{2,1,0:T(8,128)} %resid.1, ...), custom_call_target="tpu_custom_call" | custom-call | tf_op jit(solution)/shard_map/pallas_call | solution.py:514
  81.8 2.4 %shard_map.113 = (f32[1,64,512]{2,1,0:T(8,128)}, f32[1,64,512]{2,1,0:T(8,128)}, f32[1,320,512]{2,1,0:T(8,128)}) custom-call(f32[1,64,512]{2,1,0:T(8,128)} %get-tuple-element.6.stor, f32[1,64,512]{2,1,0:T(8,128)} %get-tuple-element.7.cost, bf16[320,512]{1,0:T(8,128)(2,1)} %get-tuple-element.8.network, bf16[1,320,320]{2,1,0:T(8,128)(2,1)} %inverse.3), custom_call_target="tpu_custom_call" | custom-call | tf_op jit(solution)/shard_map/pallas_call | solution.py:531

commit v6 on v5

--- a/solution.py
+++ b/solution.py
@@ -363,6 +363,7 @@
             onehot[pl.ds(pl.multiple_of((1 - core) * n, 64), n), :], state_g[t].reshape(S * 64, cols)
         ).astype(BF16)
         far_copy(inj_s.at[t, 1 - core], inj_p.at[t], injp_sem.at[t], x, 1 - core)
+    def inj_end(t):
         mine = dot(onehot[pl.ds(pl.multiple_of(core * n, 64), n), :], state_g[t].reshape(S * 64, cols))
         landed(inj_p.at[t], injp_sem.at[t])
         inj_s[t, core] = (mine + inj_p[t].astype(F32)).astype(BF16)
@@ -393,6 +394,8 @@
         full_v[t] = full.reshape(2, 64, cols)
         pend[f'full{t}'] = lambda t=t: landed(full_r.at[t], full_sem.at[t])
         far_copy(full_v.at[t, 1 - core], full_r.at[t], full_sem.at[t], x, 1 - core)
+        if t == T - 1:
+            inj_end(t)
         take(f'full{t}')
         total = full_v[t, core] + full_r[t]
         state_v[t] = total
@@ -406,6 +409,7 @@
         ring_copy(state_v.at[t], stor_out.at[0, :, lanes(x)], sout_sem.at[x], 2 * (t // 2) + core, t % 2)
         if t < T - 1:
             inj_add(t)
+            inj_end(t)
 
     for t in range(T):
         take(f'inj{t}')

time: 84.6 us -> 84.5 us (level)
  no operation moved by 1% of the time
where the time goes in v6:
time: 84.5 us; the launch traced here: 83.9 us
  Pallas kernels  83.3 us (99%)
    pallas_call x1, Pallas kernels, body(): pl.pallas_call(kernel, out_shape=(jax.ShapeDtypeStruct((1, 64, 512), F32)...  80.9 us
    pallas_call x1, Pallas kernels, body(): pl.pallas_call(finish, out_shape=(jax.ShapeDtypeStruct((1, 64, 512), F32)...  2.35 us

profile of v6, /device:TPU:7, one launch (start us, length us, event | category | flops | bytes accessed | tf_op | source)
XLA Modules:
  0.0 83.9 jit_solution(9996079795845813737)
XLA Ops:
  0.6 80.9 %shard_map.112 = (f32[1,64,512]{2,1,0:T(8,128)}, f32[1,64,512]{2,1,0:T(8,128)}, bf16[320,512]{1,0:T(8,128)(2,1)}) custom-call(bf16[1,64,2048]{2,1,0:T(8,128)(2,1)} %gain.1, bf16[1,64,2048]{2,1,0:T(8,128)(2,1)} %schur.1, bf16[1,320,320]{2,1,0:T(8,128)(2,1)} %inverse.3, bf16[320,2048]{1,0:T(8,128)(2,1)} %sens.1, f32[1,320,512]{2,1,0:T(8,128)} %resid.1, ...), custom_call_target="tpu_custom_call" | custom-call | tf_op jit(solution)/shard_map/pallas_call | solution.py:518
  81.6 2.4 %shard_map.113 = (f32[1,64,512]{2,1,0:T(8,128)}, f32[1,64,512]{2,1,0:T(8,128)}, f32[1,320,512]{2,1,0:T(8,128)}) custom-call(f32[1,64,512]{2,1,0:T(8,128)} %get-tuple-element.6.stor, f32[1,64,512]{2,1,0:T(8,128)} %get-tuple-element.7.cost, bf16[320,512]{1,0:T(8,128)(2,1)} %get-tuple-element.8.network, bf16[1,320,320]{2,1,0:T(8,128)(2,1)} %inverse.3), custom_call_target="tpu_custom_call" | custom-call | tf_op jit(solution)/shard_map/pallas_call | solution.py:535
